TPU v7x, 32 devices: a whole 2x2x4 slice. The times are simulated.
32 devices in a mesh: fsdp: 8 (over z, core), seq: 4 (over y, x).
Axes of the slice: x: 2, y: 2, z: 4, core: 2. Of those that a mesh axis runs over, the one named last changes fastest.
Arguments:
- hidden_in: bfloat16 [8192, 1536], P(('fsdp', 'seq')), may hold values from -12 to 12
- cotangent: bfloat16 [8192, 1536], P(('fsdp', 'seq')), may hold values from -6 to 6
- segment_ids: int32 [8, 1024], P('fsdp', 'seq'), may hold values from 0 to 3, never falling along the last dimension, each value on 1 to 512 neighbouring positions
- w_qkv: bfloat16 [1536, 3072], P('fsdp', 'seq'), may hold values from -1.5 to 1.5
- w_out: bfloat16 [1536, 1536], P('fsdp', 'seq'), may hold values from -0.625 to 0.625
- w_gate: bfloat16 [1536, 4096], P('fsdp', 'seq'), may hold values from -0.15625 to 0.15625
- w_up: bfloat16 [1536, 4096], P('fsdp', 'seq'), may hold values from -0.15625 to 0.15625
- w_down: bfloat16 [4096, 1536], P('fsdp', 'seq'), may hold values from -0.09375 to 0.09375
- gain_attn: bfloat16 [1536], P(('fsdp', 'seq')), may hold values from 0.099609375 to 1.8984375
- gain_mlp: bfloat16 [1536], P(('fsdp', 'seq')), may hold values from 0.099609375 to 1.8984375
Outputs:
- output: float32 [8192, 1536], P(('fsdp', 'seq'))
- d_input: float32 [8192, 1536], P(('fsdp', 'seq'))
- g_qkv: float32 [1536, 3072], P('fsdp', 'seq')
- g_out: float32 [1536, 1536], P('fsdp', 'seq')
- g_gate: float32 [1536, 4096], P('fsdp', 'seq')
- g_up: float32 [1536, 4096], P('fsdp', 'seq')
- g_down: float32 [4096, 1536], P('fsdp', 'seq')
- g_gain_attn: float32 [1536], P(('fsdp', 'seq'))
- g_gain_mlp: float32 [1536], P(('fsdp', 'seq'))
Inputs may be any that keep to these rules, and one draw needn't show every extreme that they name: `segment_ids`: document numbers never fall along a row; a document has 1 to 512 tokens.
All inputs are finite; a program needn't handle non-finite values.
Results may differ from a plain program's by a relative error of at most 0.02.
Values may be sent and summed in bfloat16 or wider, within the bound.
A program may use at most 320 MiB of HBM per device.

v0:
```python
import math

import jax
import jax.numpy as jnp
from jax import lax
from jax.sharding import PartitionSpec as P

HEAD_DIM = 96


EPSILON = 1e-05
ROPE_BASE = 100000.0
NEGATIVE = -1e30


def doc_positions(doc_ids):
    length = doc_ids.shape[0]
    tok_index = jnp.arange(length, dtype=jnp.int32)
    boundary = jnp.concatenate([jnp.ones((1,), dtype=jnp.bool_), doc_ids[1:] != doc_ids[:-1]])
    doc_start = lax.cummax(jnp.where(boundary, tok_index, jnp.zeros_like(tok_index)), axis=0)
    return tok_index - doc_start


def rope_tables(positions):
    half_dim = HEAD_DIM // 2
    freq_steps = jnp.arange(half_dim, dtype=jnp.float32)
    inverse = jnp.exp(freq_steps * (-2.0 * math.log(ROPE_BASE) / HEAD_DIM))
    angles = positions.astype(jnp.float32)[:, None] * inverse[None, :]
    return (jnp.cos(angles), jnp.sin(angles))


def rotate(block, cosine_table, sine_table):
    half_dim = block.shape[-1] // 2
    lower_part = block[..., :half_dim]
    upper_part = block[..., half_dim:]
    return jnp.concatenate(
        [
            lower_part * cosine_table - upper_part * sine_table,
            upper_part * cosine_table + lower_part * sine_table,
        ],
        axis=-1,
    )


def rotate_back(grad_in, cosine_table, sine_table):
    half_dim = grad_in.shape[-1] // 2
    lower_part = grad_in[..., :half_dim]
    upper_part = grad_in[..., half_dim:]
    return jnp.concatenate(
        [
            lower_part * cosine_table + upper_part * sine_table,
            upper_part * cosine_table - lower_part * sine_table,
        ],
        axis=-1,
    )


def inv_rms(values):
    return lax.rsqrt(jnp.mean(values * values, axis=-1, keepdims=True) + EPSILON)


def norm_back(grad_in, values, row_scale, gain_vec):
    weighted = grad_in * gain_vec
    d_values = row_scale * (
        weighted
        - values * (row_scale * row_scale) * jnp.mean(weighted * values, axis=-1, keepdims=True)
    )
    d_gain = jnp.sum(grad_in * values * row_scale, axis=0)
    return (d_values, d_gain)


def contract_rows(left, right):
    return lax.dot_general(
        left, right, (((0,), (0,)), ((), ())), preferred_element_type=jnp.float32
    )


def times_trans(left, right):
    return lax.dot_general(
        left, right, (((1,), (1,)), ((), ())), preferred_element_type=jnp.float32
    )


def block_allowed(doc_ids, block_start, block_rows):
    length = doc_ids.shape[0]
    key_index = jnp.arange(length, dtype=jnp.int32)
    query_index = block_start + jnp.arange(block_rows, dtype=jnp.int32)
    block_ids = lax.dynamic_slice_in_dim(doc_ids, block_start, block_rows, 0)
    return (block_ids[:, None] == doc_ids[None, :]) & (key_index[None, :] <= query_index[:, None])


def attend_forward(group_item, doc_ids, score_scale):
    length = group_item.shape[0]
    block_rows = min(512, length)
    queries = group_item[:, :2]
    key_rows = group_item[:, 2]
    value_rows = group_item[:, 3]

    def one_block(block_start):
        block_q = lax.dynamic_slice_in_dim(queries, block_start, block_rows, 0)
        allowed = block_allowed(doc_ids, block_start, block_rows)
        scores = (
            jnp.einsum("qhd,kd->hqk", block_q, key_rows, preferred_element_type=jnp.float32)
            * score_scale
        )
        scores = jnp.where(allowed[None], scores, NEGATIVE)
        row_max = jnp.max(scores, axis=-1, keepdims=True)
        log_total = row_max + jnp.log(jnp.sum(jnp.exp(scores - row_max), axis=-1, keepdims=True))
        weights = jnp.where(allowed[None], jnp.exp(scores - log_total), 0.0).astype(jnp.bfloat16)
        mixed_out = jnp.einsum(
            "hqk,kd->qhd", weights, value_rows, preferred_element_type=jnp.float32
        )
        return (
            mixed_out.astype(jnp.bfloat16).reshape(block_rows, 2 * HEAD_DIM),
            jnp.transpose(log_total[..., 0]),
        )

    starts = jnp.arange(length // block_rows, dtype=jnp.int32) * block_rows
    mixed_out, totals = lax.map(one_block, starts)
    return (mixed_out.reshape(length, 2 * HEAD_DIM), totals.reshape(length, 2))


def attend_backward(
    group_item, mixed_flat, totals, d_flat, doc_ids, cosine_table, sine_table, score_scale
):
    length = group_item.shape[0]
    block_rows = min(512, length)
    queries = group_item[:, :2]
    key_rows = group_item[:, 2]
    value_rows = group_item[:, 3]
    d_mixed = d_flat.reshape(length, 2, HEAD_DIM)
    row_delta = jnp.sum(
        d_mixed.astype(jnp.float32) * mixed_flat.reshape(length, 2, HEAD_DIM).astype(jnp.float32),
        axis=-1,
    )

    def one_block(running, block_start):
        d_keys, d_values = running
        block_q = lax.dynamic_slice_in_dim(queries, block_start, block_rows, 0)
        block_do = lax.dynamic_slice_in_dim(d_mixed, block_start, block_rows, 0)
        block_delta = lax.dynamic_slice_in_dim(row_delta, block_start, block_rows, 0)
        block_total = lax.dynamic_slice_in_dim(totals, block_start, block_rows, 0)
        allowed = block_allowed(doc_ids, block_start, block_rows)
        scores = (
            jnp.einsum("qhd,kd->hqk", block_q, key_rows, preferred_element_type=jnp.float32)
            * score_scale
        )
        scores = jnp.where(allowed[None], scores, NEGATIVE)
        probabilities = jnp.where(
            allowed[None], jnp.exp(scores - jnp.transpose(block_total)[:, :, None]), 0.0
        )
        d_values = d_values + jnp.einsum(
            "hqk,qhd->kd",
            probabilities.astype(jnp.bfloat16),
            block_do,
            preferred_element_type=jnp.float32,
        )
        d_probs = jnp.einsum(
            "qhd,kd->hqk", block_do, value_rows, preferred_element_type=jnp.float32
        )
        d_scores = (probabilities * (d_probs - jnp.transpose(block_delta)[:, :, None])).astype(
            jnp.bfloat16
        )
        d_query = (
            jnp.einsum("hqk,kd->qhd", d_scores, key_rows, preferred_element_type=jnp.float32)
            * score_scale
        )
        d_keys = (
            d_keys
            + jnp.einsum("hqk,qhd->kd", d_scores, block_q, preferred_element_type=jnp.float32)
            * score_scale
        )
        return ((d_keys, d_values), d_query)

    starts = jnp.arange(length // block_rows, dtype=jnp.int32) * block_rows
    zeros_kv = jnp.zeros((length, HEAD_DIM), jnp.float32)
    (d_keys, d_values), d_queries = lax.scan(one_block, (zeros_kv, zeros_kv), starts)
    d_queries = d_queries.reshape(length, 2, HEAD_DIM)
    rotated_grad = rotate_back(
        jnp.concatenate([d_queries, d_keys[:, None]], axis=1),
        cosine_table[:, None, :],
        sine_table[:, None, :],
    )
    d_packed = jnp.concatenate([rotated_grad, d_values[:, None]], axis=1).astype(jnp.bfloat16)
    return d_packed.reshape(length, 4 * HEAD_DIM)


def body(
    hidden_in, cotangent, segment_ids, w_qkv, w_out, w_gate, w_up, w_down, gain_attn, gain_mlp
):
    tok_rows = hidden_in.shape[0]
    fsdp_size = lax.axis_size("fsdp")
    seq_size = lax.axis_size("seq")
    score_scale = 1.0 / math.sqrt(HEAD_DIM)
    gain_one_shard = gain_attn.reshape(1, -1)
    gain_two_shard = gain_mlp.reshape(1, -1)
    part_qkv, part_out, part_gate, part_up, part_down, part_one, part_two = (
        lax.all_gather(w_qkv, "seq", axis=1, tiled=True),
        lax.all_gather(w_out, "seq", axis=1, tiled=True),
        lax.all_gather(w_gate, "seq", axis=1, tiled=True),
        lax.all_gather(w_up, "seq", axis=1, tiled=True),
        lax.all_gather(w_down, "seq", axis=1, tiled=True),
        lax.all_gather(gain_one_shard, "seq", axis=1, tiled=True),
        lax.all_gather(gain_two_shard, "seq", axis=1, tiled=True),
    )
    full_qkv, full_out, full_gate, full_up, full_down, full_one, full_two = (
        lax.all_gather(part_qkv, "fsdp", axis=0, tiled=True),
        lax.all_gather(part_out, "fsdp", axis=0, tiled=True),
        lax.all_gather(part_gate, "fsdp", axis=0, tiled=True),
        lax.all_gather(part_up, "fsdp", axis=0, tiled=True),
        lax.all_gather(part_down, "fsdp", axis=0, tiled=True),
        lax.all_gather(part_one, "fsdp", axis=0, tiled=True),
        lax.all_gather(part_two, "fsdp", axis=0, tiled=True),
    )
    gain_one = full_one.reshape(-1).astype(jnp.float32)
    gain_two = full_two.reshape(-1).astype(jnp.float32)
    all_ids = lax.all_gather(segment_ids, "seq", axis=1, tiled=True)[0]
    length = all_ids.shape[0]
    cosine_table, sine_table = rope_tables(doc_positions(all_ids))
    offset = lax.axis_index("seq") * tok_rows
    own_cosine = lax.dynamic_slice_in_dim(cosine_table, offset, tok_rows, 0)
    own_sine = lax.dynamic_slice_in_dim(sine_table, offset, tok_rows, 0)
    groups = full_qkv.shape[1] // (4 * HEAD_DIM)
    local_groups = groups // seq_size
    values_in = hidden_in.astype(jnp.float32)
    scale_one = inv_rms(values_in)
    normed_one = (values_in * scale_one * gain_one).astype(jnp.bfloat16)
    projected = jnp.dot(normed_one, full_qkv, preferred_element_type=jnp.float32).reshape(
        tok_rows, groups, 4, HEAD_DIM
    )
    packed = jnp.concatenate(
        [
            rotate(projected[:, :, :3], own_cosine[:, None, None, :], own_sine[:, None, None, :]),
            projected[:, :, 3:],
        ],
        axis=2,
    ).astype(jnp.bfloat16)
    packed = packed.reshape(tok_rows, seq_size, local_groups, 4 * HEAD_DIM)
    received = lax.all_to_all(packed, "seq", split_axis=1, concat_axis=0, tiled=True)
    item_count = received.shape[2]
    per_item = jnp.moveaxis(received[:, 0], 1, 0).reshape(item_count, length, 4, HEAD_DIM)
    mixed_out, totals = lax.map(
        lambda group_item: attend_forward(group_item, all_ids, score_scale), per_item
    )
    heads_mixed = jnp.moveaxis(mixed_out, 0, 1)[:, None]
    heads_total = jnp.moveaxis(totals, 0, 1)[:, None]
    attn_rows = lax.all_to_all(heads_mixed, "seq", split_axis=0, concat_axis=1, tiled=True).reshape(
        tok_rows, -1
    )
    middle = values_in + jnp.dot(attn_rows, full_out, preferred_element_type=jnp.float32)
    scale_two = inv_rms(middle)
    normed_two = (middle * scale_two * gain_two).astype(jnp.bfloat16)
    gate_pre = jnp.dot(normed_two, full_gate, preferred_element_type=jnp.float32)
    up_proj = jnp.dot(normed_two, full_up, preferred_element_type=jnp.float32)
    sigmoid_gate = jax.nn.sigmoid(gate_pre)
    activated = gate_pre * sigmoid_gate
    hidden_act = (activated * up_proj).astype(jnp.bfloat16)
    output = middle + jnp.dot(hidden_act, full_down, preferred_element_type=jnp.float32)
    cot_wide = cotangent.astype(jnp.float32)
    grad_down = contract_rows(hidden_act, cotangent)
    d_hidden = times_trans(cotangent, full_down)
    d_gate = (d_hidden * up_proj * sigmoid_gate * (1.0 + gate_pre * (1.0 - sigmoid_gate))).astype(
        jnp.bfloat16
    )
    d_up = (d_hidden * activated).astype(jnp.bfloat16)
    grad_gate = contract_rows(normed_two, d_gate)
    grad_up = contract_rows(normed_two, d_up)
    d_normed_two = times_trans(d_gate, full_gate) + times_trans(d_up, full_up)
    d_middle, grad_gain_two = norm_back(d_normed_two, middle, scale_two, gain_two)
    d_middle = cot_wide + d_middle
    d_mid_low = d_middle.astype(jnp.bfloat16)
    grad_out = contract_rows(attn_rows, d_mid_low)
    d_attn = times_trans(d_mid_low, full_out).astype(jnp.bfloat16)
    d_attn = d_attn.reshape(tok_rows, seq_size, local_groups, 2 * HEAD_DIM)
    heads_grad = lax.all_to_all(d_attn, "seq", split_axis=1, concat_axis=0, tiled=True)
    item_qkv = jnp.moveaxis(received[:, 0], 1, 0).reshape(local_groups, length, 4, HEAD_DIM)
    item_mixed = jnp.moveaxis(heads_mixed[:, 0], 1, 0)
    item_total = jnp.moveaxis(heads_total[:, 0], 1, 0)
    item_grad = jnp.moveaxis(heads_grad[:, 0], 1, 0)

    def backward_item(operands):
        group_item, mixed_flat, totals, d_flat = operands
        return attend_backward(
            group_item, mixed_flat, totals, d_flat, all_ids, cosine_table, sine_table, score_scale
        )

    d_items = lax.map(backward_item, (item_qkv, item_mixed, item_total, item_grad))
    d_heads = jnp.moveaxis(d_items, 0, 1)[:, None]
    d_packed = lax.all_to_all(d_heads, "seq", split_axis=0, concat_axis=1, tiled=True).reshape(
        tok_rows, -1
    )
    grad_qkv = contract_rows(normed_one, d_packed)
    d_normed_one = times_trans(d_packed, full_qkv)
    d_tokens, grad_gain_one = norm_back(d_normed_one, values_in, scale_one, gain_one)
    d_tokens = d_middle + d_tokens
    gain_grad_one = grad_gain_one.reshape(fsdp_size, -1)
    gain_grad_two = grad_gain_two.reshape(fsdp_size, -1)
    sum_qkv, sum_out, sum_gate, sum_up, sum_down, sum_one, sum_two = (
        lax.psum_scatter(
            grad_qkv.astype(jnp.bfloat16), "fsdp", scatter_dimension=0, tiled=True
        ).astype(jnp.float32),
        lax.psum_scatter(
            grad_out.astype(jnp.bfloat16), "fsdp", scatter_dimension=0, tiled=True
        ).astype(jnp.float32),
        lax.psum_scatter(
            grad_gate.astype(jnp.bfloat16), "fsdp", scatter_dimension=0, tiled=True
        ).astype(jnp.float32),
        lax.psum_scatter(
            grad_up.astype(jnp.bfloat16), "fsdp", scatter_dimension=0, tiled=True
        ).astype(jnp.float32),
        lax.psum_scatter(
            grad_down.astype(jnp.bfloat16), "fsdp", scatter_dimension=0, tiled=True
        ).astype(jnp.float32),
        lax.psum_scatter(
            gain_grad_one.astype(jnp.bfloat16), "fsdp", scatter_dimension=0, tiled=True
        ).astype(jnp.float32),
        lax.psum_scatter(
            gain_grad_two.astype(jnp.bfloat16), "fsdp", scatter_dimension=0, tiled=True
        ).astype(jnp.float32),
    )
    sum_qkv, sum_out, sum_gate, sum_up, sum_down, sum_one, sum_two = (
        lax.psum_scatter(
            sum_qkv.astype(jnp.bfloat16), "seq", scatter_dimension=1, tiled=True
        ).astype(jnp.float32),
        lax.psum_scatter(
            sum_out.astype(jnp.bfloat16), "seq", scatter_dimension=1, tiled=True
        ).astype(jnp.float32),
        lax.psum_scatter(
            sum_gate.astype(jnp.bfloat16), "seq", scatter_dimension=1, tiled=True
        ).astype(jnp.float32),
        lax.psum_scatter(
            sum_up.astype(jnp.bfloat16), "seq", scatter_dimension=1, tiled=True
        ).astype(jnp.float32),
        lax.psum_scatter(
            sum_down.astype(jnp.bfloat16), "seq", scatter_dimension=1, tiled=True
        ).astype(jnp.float32),
        lax.psum_scatter(
            sum_one.astype(jnp.bfloat16), "seq", scatter_dimension=1, tiled=True
        ).astype(jnp.float32),
        lax.psum_scatter(
            sum_two.astype(jnp.bfloat16), "seq", scatter_dimension=1, tiled=True
        ).astype(jnp.float32),
    )
    return (
        output,
        d_tokens,
        sum_qkv,
        sum_out,
        sum_gate,
        sum_up,
        sum_down,
        sum_one.reshape(-1),
        sum_two.reshape(-1),
    )


def solution(mesh):
    in_specs = (
        P(("fsdp", "seq"), None),
        P(("fsdp", "seq"), None),
        P("fsdp", "seq"),
        P("fsdp", "seq"),
        P("fsdp", "seq"),
        P("fsdp", "seq"),
        P("fsdp", "seq"),
        P("fsdp", "seq"),
        P(("fsdp", "seq")),
        P(("fsdp", "seq")),
    )
    out_specs = (
        P(("fsdp", "seq"), None),
        P(("fsdp", "seq"), None),
        P("fsdp", "seq"),
        P("fsdp", "seq"),
        P("fsdp", "seq"),
        P("fsdp", "seq"),
        P("fsdp", "seq"),
        P(("fsdp", "seq")),
        P(("fsdp", "seq")),
    )
    return jax.shard_map(body, mesh=mesh, in_specs=in_specs, out_specs=out_specs, check_vma=False)
```

profile of v0, /device:TPU:0, one launch (start us, length us, event | category | flops | bytes accessed | tf_op | source)
XLA Modules:
  0.0 1484.1 jit_solution(16808608916592037542)
XLA Ops:
  10.0 30.3 %all-gather.14.cloned.1.call-done = bf16[192,3072]{1,0:T(8,128)(2,1)} async-done(((bf16[192,768]{1,0:T(8,128)(2,1)}), bf16[192,3072]{1,0:T(8,128)(2,1)}) %all-gather.14.cloned.1.call-update) | async-done | bytes 1179664 | tf_op jit(solution)/shard_map/all_gather | solution.py:198
  52.7 20.5 %all-gather.20.cloned.1.call-done = bf16[192,4096]{1,0:T(8,128)(2,1)} async-done(((bf16[192,1024]{1,0:T(8,128)(2,1)}), bf16[192,4096]{1,0:T(8,128)(2,1)}) %all-gather.20.cloned.1.call-update) | async-done | bytes 1572880 | tf_op jit(solution)/shard_map/all_gather | solution.py:200
  73.3 32.8 %all-gather.24.cloned.1.call-done = bf16[192,4096]{1,0:T(8,128)(2,1)} async-done(((bf16[192,1024]{1,0:T(8,128)(2,1)}), bf16[192,4096]{1,0:T(8,128)(2,1)}) %all-gather.24.cloned.1.call-update) | async-done | bytes 1572880 | tf_op jit(solution)/shard_map/all_gather | solution.py:201
  106.1 32.5 %all-gather.28.cloned.1.call-done = bf16[512,1536]{1,0:T(8,128)(2,1)} async-done(((bf16[512,384]{1,0:T(8,128)(2,1)}), bf16[512,1536]{1,0:T(8,128)(2,1)}) %all-gather.28.cloned.1.call-update) | async-done | bytes 1572880 | tf_op jit(solution)/shard_map/all_gather | solution.py:202
  150.6 15.9 %all-reduce.9 = (bf16[1536]{0:T(1024)(128)(2,1)S(1)}, bf16[1536]{0:T(1024)(128)(2,1)}) all-reduce(bf16[1536]{0:T(1024)(128)(2,1)S(1)} %dynamic-update-slice.1, bf16[1536]{0:T(1024)(128)(2,1)S(1)} %dynamic-update-slice.3), channel_id=3, replica_groups=mesh['fsdp'=8,'seq'=4] {'fsdp'}, use_global_device_ids=true, to_apply=%add.1 | all-reduce | flops 3072 | bytes 12288
  176.6 54.8 %all-gather.16.cloned.1.call-done = bf16[1536,3072]{1,0:T(8,128)(2,1)} async-done(((bf16[192,3072]{1,0:T(8,128)(2,1)}), bf16[1536,3072]{1,0:T(8,128)(2,1)}) %all-gather.16.cloned.1.call-update) | async-done | bytes 9437200 | tf_op jit(solution)/shard_map/all_gather | solution.py:207
  243.7 19.8 %all-to-all-done = bf16[256,4,2,384]{0,3,2,1:T(8,128)(2,1)S(1)} async-done(((bf16[256,4,2,384]{0,3,2,1:T(8,128)(2,1)}), bf16[256,4,2,384]{0,3,2,1:T(8,128)(2,1)S(1)}, u32[]{:S(2)}, u32[]{:S(2)}) %all-to-all-start) | async-done | bytes 1572896 | tf_op jit(solution)/shard_map/all_to_all | solution.py:239
  265.1 34.5 %while.54 = (s32[]{:T(128)}, bf16[2,1024,192]{2,1,0:T(8,128)(2,1)}, f32[2,1024,2]{1,2,0:T(2,128)S(1)}, bf16[2,1024,4,96]{1,3,2,0:T(8,128)(2,1)S(1)}, s32[1024]{0...) while((s32[]{:T(128)}, bf16[2,1024,192]{2,1,0:T(8,128)(2,1)}, ...), condition=%wide.region_8.9_spmd, body=%wide.region_3.8_spmd.sunk | while | flops 416906752 | bytes 20773788 | solution.py:242
  265.3 16.0 %while.57 = (s32[]{:T(128)}, bf16[2,512,192]{1,2,0:T(8,128)(2,1)S(1)}, f32[2,512,2]{1,2,0:T(2,128)S(1)}, s32[2]{0:T(128)S(1)}, s32[1024]{0:T(1024)S(1)}, /*index...) while((s32[]{:T(128)}, ...), condition=%wide.region_7.7_spmd, body=%wide.region_4.6_spmd.sunk | while | flops 416906752 | bytes 15906999 | solution.py:119
  282.5 16.1 %while.57 = (s32[]{:T(128)}, bf16[2,512,192]{1,2,0:T(8,128)(2,1)S(1)}, f32[2,512,2]{1,2,0:T(2,128)S(1)}, s32[2]{0:T(128)S(1)}, s32[1024]{0:T(1024)S(1)}, /*index...) while((s32[]{:T(128)}, ...), condition=%wide.region_7.7_spmd, body=%wide.region_4.6_spmd.sunk | while | flops 416906752 | bytes 15906999 | solution.py:119
  331.6 68.8 %all-gather.22.cloned.1.call-done = bf16[1536,4096]{1,0:T(8,128)(2,1)} async-done(((bf16[192,4096]{1,0:T(8,128)(2,1)}), bf16[1536,4096]{1,0:T(8,128)(2,1)}) %all-gather.22.cloned.1.call-update) | async-done | bytes 12582928 | tf_op jit(solution)/shard_map/all_gather | solution.py:209
  409.9 107.1 %all-gather.26.cloned.1.call-done = bf16[1536,4096]{1,0:T(8,128)(2,1)} async-done(((bf16[192,4096]{1,0:T(8,128)(2,1)}), bf16[1536,4096]{1,0:T(8,128)(2,1)}) %all-gather.26.cloned.1.call-update) | async-done | bytes 12582928 | tf_op jit(solution)/shard_map/all_gather | solution.py:210
  526.6 107.1 %all-gather.30.cloned.1.call-done = bf16[4096,1536]{1,0:T(8,128)(2,1)} async-done(((bf16[512,1536]{1,0:T(8,128)(2,1)}), bf16[4096,1536]{1,0:T(8,128)(2,1)}) %all-gather.30.cloned.1.call-update) | async-done | bytes 12582928 | tf_op jit(solution)/shard_map/all_gather | solution.py:211
  690.0 103.5 %while.56 = (s32[]{:T(128)}, bf16[2,1024,384]{1,2,0:T(8,128)(2,1)}, bf16[2,1024,4,96]{1,3,2,0:T(8,128)(2,1)S(1)}, bf16[2,1024,192]{1,2,0:T(8,128)(2,1)}, bf16[2,...) while((s32[]{:T(128)}, bf16[2,1024,384]{1,2,0:T(8,128)(2,1)}, ...), condition=%wide.region_15.16_spmd.clone.clone, body=%wide.region_11.15_spmd.clone.clone.sunk | while | flops 1026292224 | bytes 83631608 | solution.py:287
  692.6 44.4 %while.58 = (s32[]{:T(128)}, f32[1024,96]{0,1:T(8,128)S(1)}, f32[1024,96]{0,1:T(8,128)}, f32[2,512,2,96]{1,0,3,2:T(2,128)}, s32[2]{0:T(128)S(1)}, /*index=5*/s32...) while((s32[]{:T(128)}, f32[1024,96]{0,1:T(8,128)S(1)}, ...), condition=%wide.region_14.14_spmd.clone, body=%wide.region_13.13_spmd.clone.sunk | while | flops 1021379072 | bytes 51358100 | solution.py:177
  744.3 44.3 %while.58 = (s32[]{:T(128)}, f32[1024,96]{0,1:T(8,128)S(1)}, f32[1024,96]{0,1:T(8,128)}, f32[2,512,2,96]{1,0,3,2:T(2,128)}, s32[2]{0:T(128)S(1)}, /*index=5*/s32...) while((s32[]{:T(128)}, f32[1024,96]{0,1:T(8,128)S(1)}, ...), condition=%wide.region_14.14_spmd.clone, body=%wide.region_13.13_spmd.clone.sunk | while | flops 1021379072 | bytes 51358100 | solution.py:177
  797.9 22.2 %all_to_all.60 = bf16[1024,1,2,384]{3,2,1,0:T(2,128)(2,1)S(1)} all-to-all(bf16[1024,1,2,384]{3,2,1,0:T(2,128)(2,1)S(1)} %bitcast.302), channel_id=1, replica_groups=mesh['fsdp'=8,'seq'=4] {'seq'}, dimensions={0} | all-to-all | bytes 3145728 | tf_op jit(solution)/shard_map/all_to_all | solution.py:289
  857.8 67.2 %reduce-scatter.17.cloned.1.call-done = bf16[192,3072]{1,0:T(8,128)(2,1)} async-done(((bf16[1536,3072]{1,0:T(8,128)(2,1)}), bf16[192,3072]{1,0:T(8,128)(2,1)}) %reduce-scatter.17.cloned.1.call-update) | async-done | bytes 1179664 | tf_op jit(solution)/shard_map/reduce_scatter | solution.py:299
  925.1 129.7 %reduce-scatter.31.cloned.1.call-done = bf16[512,1536]{1,0:T(8,128)(2,1)} async-done(((bf16[4096,1536]{1,0:T(8,128)(2,1)}), bf16[512,1536]{1,0:T(8,128)(2,1)}) %reduce-scatter.31.cloned.1.call-update) | async-done | bytes 1572880 | tf_op jit(solution)/shard_map/reduce_scatter | solution.py:311
  1057.4 127.3 %reduce-scatter.23.cloned.1.call-done = bf16[192,4096]{1,0:T(8,128)(2,1)} async-done(((bf16[1536,4096]{1,0:T(8,128)(2,1)}), bf16[192,4096]{1,0:T(8,128)(2,1)}) %reduce-scatter.23.cloned.1.call-update) | async-done | bytes 1572880 | tf_op jit(solution)/shard_map/reduce_scatter | solution.py:305
  1185.5 129.0 %reduce-scatter.27.cloned.1.call-done = bf16[192,4096]{1,0:T(8,128)(2,1)} async-done(((bf16[1536,4096]{1,0:T(8,128)(2,1)}), bf16[192,4096]{1,0:T(8,128)(2,1)}) %reduce-scatter.27.cloned.1.call-update) | async-done | bytes 1572880 | tf_op jit(solution)/shard_map/reduce_scatter | solution.py:308
  1375.4 32.0 %reduce-scatter.35.cloned.1.call-done = bf16[384,512]{1,0:T(8,128)(2,1)} async-done(((bf16[1536,512]{1,0:T(8,128)(2,1)}), bf16[384,512]{1,0:T(8,128)(2,1)}) %reduce-scatter.35.cloned.1.call-update) | async-done | bytes 393232
  1409.5 31.7 %reduce-scatter.25.cloned.1.call-done = bf16[192,1024]{1,0:T(8,128)(2,1)} async-done(((bf16[192,4096]{1,0:T(8,128)(2,1)}), bf16[192,1024]{1,0:T(8,128)(2,1)}) %reduce-scatter.25.cloned.1.call-update) | async-done | bytes 393232 | tf_op jit(solution)/shard_map/reduce_scatter | solution.py:328
  1443.2 32.0 %reduce-scatter.29.cloned.1.call-done = bf16[192,1024]{1,0:T(8,128)(2,1)} async-done(((bf16[192,4096]{1,0:T(8,128)(2,1)}), bf16[192,1024]{1,0:T(8,128)(2,1)}) %reduce-scatter.29.cloned.1.call-update) | async-done | bytes 393232 | tf_op jit(solution)/shard_map/reduce_scatter | solution.py:331
  (390 shorter events, 390.0 us)
Async XLA Ops:
  7.2 33.2 %all-gather.14.cloned.1.call-start = ((), (), s32[]{:S(2)}) async-start(), calls=%async_computation.14 | async-start | bytes 1474560 | tf_op jit(solution)/shard_map/all_gather | solution.py:198
  7.9 65.3 %all-gather.20.cloned.1.call-start = ((), (), s32[]{:S(2)}) async-start(), calls=%async_computation.17 | async-start | bytes 1966080 | tf_op jit(solution)/shard_map/all_gather | solution.py:200
  8.7 97.4 %all-gather.24.cloned.1.call-start = ((), (), s32[]{:S(2)}) async-start(), calls=%async_computation.19 | async-start | bytes 1966080 | tf_op jit(solution)/shard_map/all_gather | solution.py:201
  9.4 129.2 %all-gather.28.cloned.1.call-start = ((), (), s32[]{:S(2)}) async-start(), calls=%async_computation.21 | async-start | bytes 1966080 | tf_op jit(solution)/shard_map/all_gather | solution.py:202
  10.0 221.4 %all-gather.16.cloned.1.call-start = ((), (), s32[]{:S(2)}) async-start(), calls=%async_computation.15 | async-start | bytes 10616832 | tf_op jit(solution)/shard_map/all_gather | solution.py:207
  40.4 286.0 %all-gather.18.cloned.1.call-start = ((), (), s32[]{:S(2)}) async-start(), calls=%async_computation.16 | async-start | bytes 5308416 | tf_op jit(solution)/shard_map/all_gather | solution.py:208
  52.7 347.7 %all-gather.22.cloned.1.call-start = ((), (), s32[]{:S(2)}) async-start(), calls=%async_computation.18 | async-start | bytes 14155776 | tf_op jit(solution)/shard_map/all_gather | solution.py:209
  73.2 443.8 %all-gather.26.cloned.1.call-start = ((), (), s32[]{:S(2)}) async-start(), calls=%async_computation.20 | async-start | bytes 14155776 | tf_op jit(solution)/shard_map/all_gather | solution.py:210
  106.1 527.6 %all-gather.30.cloned.1.call-start = ((), (), s32[]{:S(2)}) async-start(), calls=%async_computation.22 | async-start | bytes 14155776 | tf_op jit(solution)/shard_map/all_gather | solution.py:211
  239.7 23.8 %all-to-all-start = ((bf16[256,4,2,384]{0,3,2,1:T(8,128)(2,1)}), bf16[256,4,2,384]{0,3,2,1:T(8,128)(2,1)S(1)}, u32[]{:S(2)}, u32[]{:S(2)}) async-start(bf16[256,4,2,384]{0,3,2,1:T(8,128)(2,1)} %bitcast.19), calls=%async_computation | async-start | bytes 3145728 | tf_op jit(solution)/shard_map/all_to_all | solution.py:239
  302.9 18.3 %all-to-all-start.1 = ((bf16[1024,1,2,192]{3,2,1,0:T(2,128)(2,1)}), bf16[1024,1,2,192]{3,2,1,0:T(2,128)(2,1)}, u32[]{:S(2)}, u32[]{:S(2)}) async-start(bf16[1024,1,2,192]{3,2,1,0:T(2,128)(2,1)} %bitcast.201), calls=%async_computation.1 | async-start | bytes 2097152 | tf_op jit(solution)/shard_map/all_to_all | solution.py:247
  331.6 185.4 %copy-start.15 = (bf16[256,1536]{1,0:T(8,128)(2,1)}, bf16[256,1536]{1,0:T(8,128)(2,1)S(1)}, u32[]{:S(2)}) copy-start(bf16[256,1536]{1,0:T(8,128)(2,1)S(1)} %multiply_convert_fusion.3) | copy-start | bytes 2359300
  671.0 15.8 %all-to-all-start.2 = ((bf16[256,4,2,192]{0,3,2,1:T(8,128)(2,1)}), bf16[256,4,2,192]{0,3,2,1:T(8,128)(2,1)}, u32[]{:S(2)}, u32[]{:S(2)}) async-start(bf16[256,4,2,192]{0,3,2,1:T(8,128)(2,1)} %bitcast.31), calls=%async_computation.2 | async-start | bytes 1572864 | tf_op jit(solution)/shard_map/all_to_all | solution.py:275
  675.2 180.2 %reduce-scatter.21.cloned.1.call-start = ((), (), s32[]{:S(2)}) async-start(), calls=%async_computation.25 | async-start | bytes 5308416 | tf_op jit(solution)/shard_map/reduce_scatter | solution.py:302
  681.8 243.2 %reduce-scatter.17.cloned.1.call-start = ((), (), s32[]{:S(2)}) async-start(), calls=%async_computation.23 | async-start | bytes 10616832 | tf_op jit(solution)/shard_map/reduce_scatter | solution.py:299
  828.6 226.1 %reduce-scatter.31.cloned.1.call-start = ((), (), s32[]{:S(2)}) async-start(), calls=%async_computation.30 | async-start | bytes 14155776 | tf_op jit(solution)/shard_map/reduce_scatter | solution.py:311
  837.7 346.9 %reduce-scatter.23.cloned.1.call-start = ((), (), s32[]{:S(2)}) async-start(), calls=%async_computation.26 | async-start | bytes 14155776 | tf_op jit(solution)/shard_map/reduce_scatter | solution.py:305
  847.3 467.2 %reduce-scatter.27.cloned.1.call-start = ((), (), s32[]{:S(2)}) async-start(), calls=%async_computation.28 | async-start | bytes 14155776 | tf_op jit(solution)/shard_map/reduce_scatter | solution.py:308
  855.4 504.5 %reduce-scatter.33.cloned.1.call-start = ((), (), s32[]{:S(2)}) async-start(), calls=%async_computation.31 | async-start | bytes 983040
  857.7 515.9 %reduce-scatter.19.cloned.1.call-start = ((), (), s32[]{:S(2)}) async-start(), calls=%async_computation.24 | async-start | bytes 1474560 | tf_op jit(solution)/shard_map/reduce_scatter | solution.py:322
  925.0 482.4 %reduce-scatter.35.cloned.1.call-start = ((), (), s32[]{:S(2)}) async-start(), calls=%async_computation.32 | async-start | bytes 1966080
  1057.3 257.1 %copy-start.12 = (f32[256,1536]{1,0:T(8,128)S(1)}, f32[256,1536]{1,0:T(8,128)}, u32[]{:S(2)}) copy-start(f32[256,1536]{1,0:T(8,128)} %copy-done.10) | copy-start | bytes 4718596
  1057.3 383.9 %reduce-scatter.25.cloned.1.call-start = ((), (), s32[]{:S(2)}) async-start(), calls=%async_computation.27 | async-start | bytes 1966080 | tf_op jit(solution)/shard_map/reduce_scatter | solution.py:328
  1184.7 290.5 %reduce-scatter.29.cloned.1.call-start = ((), (), s32[]{:S(2)}) async-start(), calls=%async_computation.29 | async-start | bytes 1966080 | tf_op jit(solution)/shard_map/reduce_scatter | solution.py:331
  (61 other events, 1034.2 us)
Sparse Core Ops, SparseCore 0:
  9.9 30.4 all-gather.13
  42.2 30.9 all-gather.19
  75.0 30.9 all-gather.23
  107.7 30.8 all-gather.27
  140.1 91.2 all-gather.15
  232.9 50.1 all-gather.17
  284.8 115.5 all-gather.21
  402.0 114.9 all-gather.25
  518.6 114.9 all-gather.29
  681.9 53.6 reduce-scatter.20
  828.7 96.2 reduce-scatter.16
  927.1 127.5 reduce-scatter.30
  1057.0 127.5 reduce-scatter.22
  1186.8 127.5 reduce-scatter.26
  1317.7 24.4 reduce-scatter.32
  1345.0 28.5 reduce-scatter.18
  1376.4 30.9 reduce-scatter.34
  1410.2 30.9 reduce-scatter.24
  1444.2 30.8 reduce-scatter.28
where the time goes:
time: 1490 us; the launch traced here: 1480 us
  waiting for transfers between devices  1060 us (71%)
  matrix products  161 us (11%)
  local copies, waits for them, and re-layouts  93.3 us (6%)
  blocking collectives  91.4 us (6%)
  other arithmetic  36 us (2%)
  between operations  16.9 us (1%)
  loops' own time  16.7 us (1%)
    reduce_scatter x1, waiting for transfers between devices, body(): lax.psum_scatter(grad_down.astype(jnp.bfloat16), 'fsdp', scatter_dimensio...  130 us
    reduce_scatter x1, waiting for transfers between devices, body(): lax.psum_scatter(grad_up.astype(jnp.bfloat16), 'fsdp', scatter_dimension=...  129 us
    reduce_scatter x1, waiting for transfers between devices, body(): lax.psum_scatter(grad_gate.astype(jnp.bfloat16), 'fsdp', scatter_dimensio...  127 us
    all_gather x1, waiting for transfers between devices, body(): lax.all_gather(part_down, 'fsdp', axis=0, tiled=True)  107 us
    all_gather x1, waiting for transfers between devices, body(): lax.all_gather(part_up, 'fsdp', axis=0, tiled=True)  107 us
    all_gather x1, waiting for transfers between devices, body(): lax.all_gather(part_gate, 'fsdp', axis=0, tiled=True)  68.8 us
    reduce_scatter x1, waiting for transfers between devices, body(): lax.psum_scatter(grad_qkv.astype(jnp.bfloat16), 'fsdp', scatter_dimension...  67.2 us
    all_gather x1, waiting for transfers between devices, body(): lax.all_gather(part_qkv, 'fsdp', axis=0, tiled=True)  54.8 us
  transfers between devices with their start and end apart: 22, of which 19 were waited for; matrix products, arithmetic and copies ran while one was open for 16% of the time, Pallas kernels for 0%

commit v1 on v0

v1 whole, which is shorter than its diff:
```python
import math

import jax
import jax.numpy as jnp
from jax import lax
from jax.sharding import PartitionSpec as P

HEAD_DIM = 96
EPSILON = 1e-05
ROPE_BASE = 100000.0
NEGATIVE = -1e30


def rope_tables(ids):
    length = ids.shape[0]
    first = jnp.sum((ids[None, :] < ids[:, None]).astype(jnp.int32), axis=1)
    positions = jnp.arange(length, dtype=jnp.int32) - first
    half_dim = HEAD_DIM // 2
    freq_steps = jnp.arange(half_dim, dtype=jnp.float32)
    inverse = jnp.exp(freq_steps * (-2.0 * math.log(ROPE_BASE) / HEAD_DIM))
    angles = positions.astype(jnp.float32)[:, None] * inverse[None, :]
    return (jnp.cos(angles), jnp.sin(angles))


def rotate(block, cosine_table, sine_table):
    half_dim = block.shape[-1] // 2
    lower, upper = block[..., :half_dim], block[..., half_dim:]
    return jnp.concatenate(
        [lower * cosine_table - upper * sine_table, upper * cosine_table + lower * sine_table],
        axis=-1,
    )


def inv_rms(values):
    return lax.rsqrt(jnp.mean(values * values, axis=-1, keepdims=True) + EPSILON)


def norm_back(grad_in, values, row_scale, gain_vec):
    weighted = grad_in * gain_vec
    d_values = row_scale * (
        weighted
        - values * (row_scale * row_scale) * jnp.mean(weighted * values, axis=-1, keepdims=True)
    )
    return (d_values, jnp.sum(grad_in * values * row_scale, axis=0))


def contract_rows(left, right):
    return lax.dot_general(
        left, right, (((0,), (0,)), ((), ())), preferred_element_type=jnp.float32
    )


def times(left, right):
    return jnp.dot(left, right, preferred_element_type=jnp.float32)


def times_trans(left, right):
    return lax.dot_general(
        left, right, (((1,), (1,)), ((), ())), preferred_element_type=jnp.float32
    )


def attend_forward(group, allowed, score_scale):
    queries, keys, vals = group[:, :2], group[:, 2], group[:, 3]
    scores = jnp.einsum("qhd,kd->hqk", queries, keys, preferred_element_type=jnp.float32)
    scores = jnp.where(allowed[None], scores * score_scale, NEGATIVE)
    row_max = jnp.max(scores, axis=-1, keepdims=True)
    lse = row_max + jnp.log(jnp.sum(jnp.exp(scores - row_max), axis=-1, keepdims=True))
    weights = jnp.where(allowed[None], jnp.exp(scores - lse), 0.0).astype(jnp.bfloat16)
    mixed = jnp.einsum("hqk,kd->qhd", weights, vals, preferred_element_type=jnp.float32)
    return mixed.astype(jnp.bfloat16), lse


def attend_backward(group, mixed, lse, d_mixed, allowed, score_scale):
    queries, keys, vals = group[:, :2], group[:, 2], group[:, 3]
    delta = jnp.sum(d_mixed.astype(jnp.float32) * mixed.astype(jnp.float32), axis=-1)
    scores = jnp.einsum("qhd,kd->hqk", queries, keys, preferred_element_type=jnp.float32)
    probs = jnp.where(allowed[None], jnp.exp(scores * score_scale - lse), 0.0)
    d_vals = jnp.einsum(
        "hqk,qhd->kd", probs.astype(jnp.bfloat16), d_mixed, preferred_element_type=jnp.float32
    )
    d_probs = jnp.einsum("qhd,kd->hqk", d_mixed, vals, preferred_element_type=jnp.float32)
    d_scores = (probs * (d_probs - jnp.transpose(delta)[:, :, None])).astype(jnp.bfloat16)
    d_q = jnp.einsum("hqk,kd->qhd", d_scores, keys, preferred_element_type=jnp.float32)
    d_k = jnp.einsum("hqk,qhd->kd", d_scores, queries, preferred_element_type=jnp.float32)
    return d_q * score_scale, d_k * score_scale, d_vals


def body(
    hidden_in, cotangent, segment_ids, w_qkv, w_out, w_gate, w_up, w_down, gain_attn, gain_mlp
):
    rows = hidden_in.shape[0]
    fsdp = lax.axis_size("fsdp")
    seq = lax.axis_size("seq")
    ratio = fsdp // seq
    scale = 1.0 / math.sqrt(HEAD_DIM)
    length = rows * seq
    moves = [
        (f * seq + s, ((f % ratio) * seq + s) * seq + f // ratio)
        for f in range(fsdp)
        for s in range(seq)
    ]
    back = [(there, here) for here, there in moves]

    def gather_rows(shard):
        height, width = shard.shape
        moved = lax.ppermute(shard, ("fsdp", "seq"), moves)
        blocks = lax.all_gather(moved, "fsdp", axis=0, tiled=False)
        blocks = blocks.reshape(ratio, seq, height, width)
        return jnp.transpose(blocks, (0, 2, 1, 3)).reshape(ratio * height, seq * width)

    def scatter_rows(grad):
        height, width = grad.shape[0] // ratio, grad.shape[1] // seq
        blocks = grad.astype(jnp.bfloat16).reshape(ratio, height, seq, width)
        blocks = jnp.transpose(blocks, (0, 2, 1, 3)).reshape(fsdp, height, width)
        own = lax.psum_scatter(blocks, "fsdp", scatter_dimension=0, tiled=False)
        return lax.ppermute(own, ("fsdp", "seq"), back).astype(jnp.float32)

    def gather_cols(shard):
        return lax.all_gather(shard, "fsdp", axis=0, tiled=True)

    def scatter_cols(grad):
        return lax.psum_scatter(
            grad.astype(jnp.bfloat16), "fsdp", scatter_dimension=0, tiled=True
        ).astype(jnp.float32)

    def gather_tokens(block):
        return lax.all_gather(block, "seq", axis=0, tiled=True)

    def scatter_tokens(partial):
        return lax.psum_scatter(
            partial.astype(jnp.bfloat16), "seq", scatter_dimension=0, tiled=True
        ).astype(jnp.float32)

    gains = lax.all_gather(
        jnp.stack([gain_attn, gain_mlp]), ("fsdp", "seq"), axis=1, tiled=True
    ).astype(jnp.float32)
    gain_one, gain_two = gains[0], gains[1]
    ids = lax.all_gather(segment_ids, "seq", axis=1, tiled=True)[0]
    hidden_all = gather_tokens(hidden_in)
    cot_all = gather_tokens(cotangent)
    cols_qkv = gather_cols(w_qkv)
    rows_out = gather_rows(w_out)
    cols_gate = gather_cols(w_gate)
    cols_up = gather_cols(w_up)
    rows_down = gather_rows(w_down)

    tok = jnp.arange(length, dtype=jnp.int32)
    allowed = (ids[:, None] == ids[None, :]) & (tok[None, :] <= tok[:, None])
    cosine, sine = rope_tables(ids)

    values_all = hidden_all.astype(jnp.float32)
    normed_one = (values_all * inv_rms(values_all) * gain_one).astype(jnp.bfloat16)
    groups = cols_qkv.shape[1] // (4 * HEAD_DIM)
    projected = times(normed_one, cols_qkv).reshape(length, groups, 4, HEAD_DIM)
    packed = jnp.concatenate(
        [
            rotate(projected[:, :, :3], cosine[:, None, None, :], sine[:, None, None, :]),
            projected[:, :, 3:],
        ],
        axis=2,
    ).astype(jnp.bfloat16)
    forward = [attend_forward(packed[:, g], allowed, scale) for g in range(groups)]
    attn = jnp.stack([mixed for mixed, _ in forward], axis=1).reshape(length, -1)

    values_in = hidden_in.astype(jnp.float32)
    middle = values_in + scatter_tokens(times(attn, rows_out))
    scale_two = inv_rms(middle)
    normed_two = gather_tokens((middle * scale_two * gain_two).astype(jnp.bfloat16))
    gate = times(normed_two, cols_gate)
    up = times(normed_two, cols_up)
    sig = jax.nn.sigmoid(gate)
    activated = gate * sig
    hid = (activated * up).astype(jnp.bfloat16)
    output = middle + scatter_tokens(times(hid, rows_down))
    g_down = scatter_rows(contract_rows(hid, cot_all))
    d_hid = times_trans(cot_all, rows_down)
    d_gate = (d_hid * up * sig * (1.0 + gate * (1.0 - sig))).astype(jnp.bfloat16)
    d_up = (d_hid * activated).astype(jnp.bfloat16)
    g_gate = scatter_cols(contract_rows(normed_two, d_gate))
    g_up = scatter_cols(contract_rows(normed_two, d_up))
    d_normed_two = scatter_tokens(times_trans(d_gate, cols_gate) + times_trans(d_up, cols_up))
    d_middle, part_two = norm_back(d_normed_two, middle, scale_two, gain_two)
    d_middle = cotangent.astype(jnp.float32) + d_middle
    d_low = gather_tokens(d_middle.astype(jnp.bfloat16))
    g_out = scatter_rows(contract_rows(attn, d_low))
    d_attn = times_trans(d_low, rows_out).astype(jnp.bfloat16)
    d_attn = d_attn.reshape(length, groups, 2, HEAD_DIM)
    pieces = []
    for g in range(groups):
        d_q, d_k, d_v = attend_backward(
            packed[:, g], forward[g][0], forward[g][1], d_attn[:, g], allowed, scale
        )
        turned = rotate(
            jnp.concatenate([d_q, d_k[:, None]], axis=1), cosine[:, None, :], -sine[:, None, :]
        )
        pieces.append(jnp.concatenate([turned, d_v[:, None]], axis=1))
    d_packed = jnp.stack(pieces, axis=1).reshape(length, -1).astype(jnp.bfloat16)
    g_qkv = scatter_cols(contract_rows(normed_one, d_packed))
    d_normed_one = scatter_tokens(times_trans(d_packed, cols_qkv))
    d_tokens, part_one = norm_back(d_normed_one, values_in, inv_rms(values_in), gain_one)
    d_tokens = d_middle + d_tokens
    g_gains = lax.psum_scatter(
        jnp.stack([part_one, part_two]), ("fsdp", "seq"), scatter_dimension=1, tiled=True
    )
    return (output, d_tokens, g_qkv, g_out, g_gate, g_up, g_down, g_gains[0], g_gains[1])


def solution(mesh):
    both = P(("fsdp", "seq"), None)
    split = P("fsdp", "seq")
    gain = P(("fsdp", "seq"))
    in_specs = (both, both, split, split, split, split, split, split, gain, gain)
    out_specs = (both, both, split, split, split, split, split, gain, gain)
    return jax.shard_map(body, mesh=mesh, in_specs=in_specs, out_specs=out_specs, check_vma=False)
```

time: 1490 us -> 960 us (0.64)
  waiting for transfers between devices: 1060 us -> 643 us
  local copies, waits for them, and re-layouts: 93.3 us -> 34.7 us
  matrix products: 161 us -> 134 us
  loops' own time: 16.7 us -> 0 us
    all_gather x9, waiting for transfers between devices: 454 us -> 211 us  [the longest x4 92.2 us: gather_tokens(): return lax.all_gather(block, 'seq', axis=0, tiled=True)]
    reduce_scatter x8 -> x9, waiting for transfers between devices: 529 us -> 332 us  [the longest x4 181 us: scatter_tokens(): lax.psum_scatter(partial.astype(jnp.bfloat16), 'seq', scatter_dimension=0...]
    unnamed x21 -> x20, waiting for transfers between devices: 34.8 us -> 100 us
    all_gather x2, blocking collectives: 20.2 us -> 81.8 us  [the longest x1 74.6 us: body(): lax.all_gather(jnp.stack([gain_attn, gain_mlp]), ('fsdp', 'seq'), axis=1,...]
    unnamed x4 -> x0, blocking collectives: 49 us -> none
    all_to_all x3 -> x0, waiting for transfers between devices: 38.3 us -> none  [the longest x1 19.8 us: body(): lax.all_to_all(packed, 'seq', split_axis=1, concat_axis=0, tiled=True)]
    dynamic_update_slice x18 -> x0, local copies, waits for them, and re-layouts: 37.6 us -> none  [the longest x8 33.9 us: attend_backward(): lax.scan(one_block, (zeros_kv, zeros_kv), starts)]
    all_to_all x1 -> x0, blocking collectives: 22.2 us -> none  [body(): lax.all_to_all(d_heads, 'seq', split_axis=0, concat_axis=1, tiled=True)]
  transfers between devices with their start and end apart: 22 -> 23, of which waited for: 19 -> 16; matrix products, arithmetic and copies ran while one was open for 16% -> 15% of each run, Pallas kernels for 0% -> 0%
where the time goes in v1:
time: 960 us; the launch traced here: 949 us
  waiting for transfers between devices  643 us (67%)
  matrix products  134 us (14%)
  blocking collectives  81.8 us (9%)
  other arithmetic  34.8 us (4%)
  local copies, waits for them, and re-layouts  34.7 us (4%)
  between operations  15 us (2%)
    reduce_scatter x4, waiting for transfers between devices, scatter_tokens(): lax.psum_scatter(partial.astype(jnp.bfloat16), 'seq', scatter_dimension=0...  181 us
    reduce_scatter x3, waiting for transfers between devices, scatter_cols(): lax.psum_scatter(grad.astype(jnp.bfloat16), 'fsdp', scatter_dimension=0,...  118 us
    unnamed x20, waiting for transfers between devices  100 us
    all_gather x4, waiting for transfers between devices, gather_tokens(): return lax.all_gather(block, 'seq', axis=0, tiled=True)  92.2 us
    all_gather x3, waiting for transfers between devices, gather_cols(): return lax.all_gather(shard, 'fsdp', axis=0, tiled=True)  83.8 us
    all_gather x1, blocking collectives, body(): lax.all_gather(jnp.stack([gain_attn, gain_mlp]), ('fsdp', 'seq'), axis=1,...  74.6 us
    all_gather x2, waiting for transfers between devices, gather_rows(): blocks = lax.all_gather(moved, 'fsdp', axis=0, tiled=False)  34.8 us
    dot_general x5, matrix products, times(): return jnp.dot(left, right, preferred_element_type=jnp.float32)  33.2 us
  transfers between devices with their start and end apart: 23, of which 16 were waited for; matrix products, arithmetic and copies ran while one was open for 15% of the time, Pallas kernels for 0%

profile of v1, /device:TPU:0, one launch (start us, length us, event | category | flops | bytes accessed | tf_op | source)
XLA Modules:
  0.0 949.4 jit_solution(4358844575518664176)
XLA Ops:
  11.7 74.6 %all-gather.2 = bf16[32,48,2]{1,2,0:T(2,128)(2,1)S(1)} all-gather(bf16[1,48,2]{1,2,0:T(2,128)(2,1)S(1)} %maximum_bitcast_fusion.2), channel_id=1, replica_groups=mesh['fsdp'=8,'seq'=4] {'fsdp','seq'}, dimensions={0}, use_global_device_ids=true | all-gather | bytes 6336 | tf_op jit(solution)/shard_map/all_gather | solution.py:135
  102.6 20.0 %all-gather.15.cloned.1.call-done = bf16[1536,768]{1,0:T(8,128)(2,1)} async-done(((bf16[192,768]{1,0:T(8,128)(2,1)}), bf16[1536,768]{1,0:T(8,128)(2,1)}) %all-gather.15.cloned.1.call-update) | async-done | bytes 2359312 | tf_op jit(solution)/shard_map/all_gather | solution.py:120
  151.5 47.1 %reduce-scatter.13.cloned.1.call-done = bf16[256,1536]{1,0:T(8,128)(2,1)} async-done(((bf16[1024,1536]{1,0:T(8,128)(2,1)}), bf16[256,1536]{1,0:T(8,128)(2,1)}) %reduce-scatter.13.cloned.1.call-update) | async-done | bytes 786448 | tf_op jit(solution)/shard_map/reduce_scatter | solution.py:131
  204.2 34.8 %all-gather.29.cloned.1.call-done = bf16[4096,384]{1,0:T(8,128)(2,1)} async-done(((bf16[512,384]{1,0:T(8,128)(2,1)}), bf16[4096,384]{1,0:T(8,128)(2,1)}) %all-gather.29.cloned.1.call-update) | async-done | bytes 3145744 | tf_op jit(solution)/shard_map/all_gather | solution.py:108
  245.5 32.1 %all-gather.21.cloned.1.call-done = bf16[1536,1024]{1,0:T(8,128)(2,1)} async-done(((bf16[192,1024]{1,0:T(8,128)(2,1)}), bf16[1536,1024]{1,0:T(8,128)(2,1)}) %all-gather.21.cloned.1.call-update) | async-done | bytes 3145744 | tf_op jit(solution)/shard_map/all_gather | solution.py:120
  277.6 45.3 %all-gather.17.cloned.1.call-done = bf16[1024,1536]{1,0:T(8,128)(2,1)} async-done(((bf16[256,1536]{1,0:T(8,128)(2,1)}), bf16[1024,1536]{1,0:T(8,128)(2,1)}) %all-gather.17.cloned.1.call-update) | async-done | bytes 3145744 | tf_op jit(solution)/shard_map/all_gather | solution.py:128
  322.9 8.3 fusion.95
  331.2 31.7 %all-gather.19.cloned.1.call-done = bf16[1536,1024]{1,0:T(8,128)(2,1)} async-done(((bf16[192,1024]{1,0:T(8,128)(2,1)}), bf16[1536,1024]{1,0:T(8,128)(2,1)}) %all-gather.19.cloned.1.call-update) | async-done | bytes 3145744 | tf_op jit(solution)/shard_map/all_gather | solution.py:120
  362.9 8.2 fusion.94
  371.1 36.5 %all-gather.23.cloned.1.call-done = bf16[1024,1536]{1,0:T(8,128)(2,1)} async-done(((bf16[256,1536]{1,0:T(8,128)(2,1)}), bf16[1024,1536]{1,0:T(8,128)(2,1)}) %all-gather.23.cloned.1.call-update) | async-done | bytes 3145744 | tf_op jit(solution)/shard_map/all_gather | solution.py:128
  407.6 11.6 %multiply_convert_fusion = (bf16[1024,1024]{1,0:T(8,128)(2,1)S(1)}, bf16[1024,1024]{1,0:T(8,128)(2,1)S(1)}, bf16[1024,1024]{1,0:T(8,128)(2,1)}) fusion(f32[1024,1024]{1,0:T(8,128)} %fusion.94, f32[1024,1024]{1,0:T(8,128)} %fusion.95, bf16[1024,1536]{1,0:T(8,128)(2,1)} %all-gather.23.cloned.1.call-done, bf16[1024,1536]{1,0:T(8,128)(2,1)} %bitcast.230), kind=kOutput, calls=%fused_computation.28 | convolution fusion | flops 3236954112 | bytes 20971520 | tf_op jit(solution)/shard_map/dot_general | solution.py:58
  428.2 44.1 %reduce-scatter.17.cloned.1.call-done = bf16[256,1536]{1,0:T(8,128)(2,1)} async-done(((bf16[1024,1536]{1,0:T(8,128)(2,1)}), bf16[256,1536]{1,0:T(8,128)(2,1)}) %reduce-scatter.17.cloned.1.call-update) | async-done | bytes 786448 | tf_op jit(solution)/shard_map/reduce_scatter | solution.py:131
  477.5 7.6 convolution_convert_fusion.2
  495.4 7.7 convolution_convert_fusion.3
  503.2 7.7 convolution_convert_fusion.4
  511.2 10.4 %all-gather.25.cloned.1.call-done = bf16[1024,1536]{1,0:T(8,128)(2,1)} async-done(((bf16[256,1536]{1,0:T(8,128)(2,1)}), bf16[1024,1536]{1,0:T(8,128)(2,1)}) %all-gather.25.cloned.1.call-update) | async-done | bytes 3145744 | tf_op jit(solution)/shard_map/all_gather | solution.py:128
  575.4 7.7 convolution_convert_fusion.5
  585.5 42.7 %reduce-scatter.27.cloned.1.call-done = bf16[192,1024]{1,0:T(8,128)(2,1)} async-done(((bf16[1536,1024]{1,0:T(8,128)(2,1)}), bf16[192,1024]{1,0:T(8,128)(2,1)}) %reduce-scatter.27.cloned.1.call-update) | async-done | bytes 393232 | tf_op jit(solution)/shard_map/reduce_scatter | solution.py:123
  630.1 42.7 %reduce-scatter.25.cloned.1.call-done = bf16[192,1024]{1,0:T(8,128)(2,1)} async-done(((bf16[1536,1024]{1,0:T(8,128)(2,1)}), bf16[192,1024]{1,0:T(8,128)(2,1)}) %reduce-scatter.25.cloned.1.call-update) | async-done | bytes 393232 | tf_op jit(solution)/shard_map/reduce_scatter | solution.py:123
  674.7 32.7 %reduce-scatter.23.cloned.1.call-done = bf16[1,192,384]{2,1,0:T(8,128)(2,1)} async-done(((bf16[8,192,384]{2,1,0:T(8,128)(2,1)}), bf16[1,192,384]{2,1,0:T(8,128)(2,1)}) %reduce-scatter.23.cloned.1.call-update) | async-done | bytes 147472 | tf_op jit(solution)/shard_map/reduce_scatter | solution.py:116
  711.9 32.5 %reduce-scatter.21.cloned.1.call-done = bf16[192,768]{1,0:T(8,128)(2,1)} async-done(((bf16[1536,768]{1,0:T(8,128)(2,1)}), bf16[192,768]{1,0:T(8,128)(2,1)}) %reduce-scatter.21.cloned.1.call-update) | async-done | bytes 294928 | tf_op jit(solution)/shard_map/reduce_scatter | solution.py:123
  746.3 46.9 %reduce-scatter.19.cloned.1.call-done = bf16[256,1536]{1,0:T(8,128)(2,1)} async-done(((bf16[1024,1536]{1,0:T(8,128)(2,1)}), bf16[256,1536]{1,0:T(8,128)(2,1)}) %reduce-scatter.19.cloned.1.call-update) | async-done | bytes 786448 | tf_op jit(solution)/shard_map/reduce_scatter | solution.py:131
  796.7 43.3 %reduce-scatter.15.cloned.1.call-done = bf16[256,1536]{1,0:T(8,128)(2,1)} async-done(((bf16[1024,1536]{1,0:T(8,128)(2,1)}), bf16[256,1536]{1,0:T(8,128)(2,1)}) %reduce-scatter.15.cloned.1.call-update) | async-done | bytes 786448 | tf_op jit(solution)/shard_map/reduce_scatter | solution.py:131
  844.1 96.5 %reduce-scatter.31.cloned.1.call-done = f32[48,2]{1,0:T(8,128)} async-done(((f32[1536,2]{1,0:T(8,128)}), f32[48,2]{1,0:T(8,128)}) %reduce-scatter.31.cloned.1.call-update) | async-done | bytes 400
  (228 shorter events, 161.8 us)
Async XLA Ops:
  7.2 89.1 %all-gather.27.cloned.1.call-start = ((), (), s32[]{:S(2)}) async-start(), calls=%async_computation.26 | async-start | bytes 1327104 | tf_op jit(solution)/shard_map/all_gather | solution.py:108
  7.2 1.6 collective-permute-start
  9.5 90.5 %all-gather.13.cloned.1.call-start = ((), (), s32[]{:S(2)}) async-start(), calls=%async_computation.10 | async-start | bytes 3932160 | tf_op jit(solution)/shard_map/all_gather | solution.py:128
  10.2 112.4 %all-gather.15.cloned.1.call-start = ((), (), s32[]{:S(2)}) async-start(), calls=%async_computation.11 | async-start | bytes 2654208 | tf_op jit(solution)/shard_map/all_gather | solution.py:120
  11.0 187.6 %reduce-scatter.13.cloned.1.call-start = ((), (), s32[]{:S(2)}) async-start(), calls=%async_computation.12 | async-start | bytes 3932160 | tf_op jit(solution)/shard_map/reduce_scatter | solution.py:131
  128.9 415.6 %copy-start.10 = (bf16[1024,4,96]{0,2,1:T(8,128)(2,1)}, bf16[1024,4,96]{0,2,1:T(8,128)(2,1)S(1)}, u32[]{:S(2)}) copy-start(bf16[1024,4,96]{0,2,1:T(8,128)(2,1)S(1)} %get-tuple-element.32) | copy-start | bytes 2359300
  148.4 90.5 %all-gather.29.cloned.1.call-start = ((), (), s32[]{:S(2)}) async-start(), calls=%async_computation.27 | async-start | bytes 3538944 | tf_op jit(solution)/shard_map/all_gather | solution.py:108
  149.4 0.7 collective-permute-start.1
  150.9 126.8 %all-gather.21.cloned.1.call-start = ((), (), s32[]{:S(2)}) async-start(), calls=%async_computation.15 | async-start | bytes 3538944 | tf_op jit(solution)/shard_map/all_gather | solution.py:120
  151.4 171.5 %all-gather.17.cloned.1.call-start = ((), (), s32[]{:S(2)}) async-start(), calls=%async_computation.13 | async-start | bytes 3932160 | tf_op jit(solution)/shard_map/all_gather | solution.py:128
  202.4 160.5 %all-gather.19.cloned.1.call-start = ((), (), s32[]{:S(2)}) async-start(), calls=%async_computation.14 | async-start | bytes 3538944 | tf_op jit(solution)/shard_map/all_gather | solution.py:120
  203.2 204.4 %all-gather.23.cloned.1.call-start = ((), (), s32[]{:S(2)}) async-start(), calls=%async_computation.17 | async-start | bytes 3932160 | tf_op jit(solution)/shard_map/all_gather | solution.py:128
  203.9 268.4 %reduce-scatter.17.cloned.1.call-start = ((), (), s32[]{:S(2)}) async-start(), calls=%async_computation.18 | async-start | bytes 3932160 | tf_op jit(solution)/shard_map/reduce_scatter | solution.py:131
  428.2 93.4 %all-gather.25.cloned.1.call-start = ((), (), s32[]{:S(2)}) async-start(), calls=%async_computation.19 | async-start | bytes 3932160 | tf_op jit(solution)/shard_map/all_gather | solution.py:128
  477.5 105.7 %reduce-scatter.29.cloned.1.call-start = ((), (), s32[]{:S(2)}) async-start(), calls=%async_computation.25 | async-start | bytes 3538944 | tf_op jit(solution)/shard_map/reduce_scatter | solution.py:116
  495.4 132.7 %reduce-scatter.27.cloned.1.call-start = ((), (), s32[]{:S(2)}) async-start(), calls=%async_computation.24 | async-start | bytes 3538944 | tf_op jit(solution)/shard_map/reduce_scatter | solution.py:123
  503.1 169.6 %reduce-scatter.25.cloned.1.call-start = ((), (), s32[]{:S(2)}) async-start(), calls=%async_computation.23 | async-start | bytes 3538944 | tf_op jit(solution)/shard_map/reduce_scatter | solution.py:123
  510.9 196.5 %reduce-scatter.23.cloned.1.call-start = ((), (), s32[]{:S(2)}) async-start(), calls=%async_computation.22 | async-start | bytes 1327104 | tf_op jit(solution)/shard_map/reduce_scatter | solution.py:116
  549.4 195.1 %reduce-scatter.21.cloned.1.call-start = ((), (), s32[]{:S(2)}) async-start(), calls=%async_computation.21 | async-start | bytes 2654208 | tf_op jit(solution)/shard_map/reduce_scatter | solution.py:123
  569.6 223.6 %reduce-scatter.19.cloned.1.call-start = ((), (), s32[]{:S(2)}) async-start(), calls=%async_computation.20 | async-start | bytes 3932160 | tf_op jit(solution)/shard_map/reduce_scatter | solution.py:131
  575.4 264.6 %reduce-scatter.15.cloned.1.call-start = ((), (), s32[]{:S(2)}) async-start(), calls=%async_computation.16 | async-start | bytes 3932160 | tf_op jit(solution)/shard_map/reduce_scatter | solution.py:131
  583.1 357.5 %reduce-scatter.31.cloned.1.call-start = ((), (), s32[]{:S(2)}) async-start(), calls=%async_computation.28 | async-start | bytes 811008
  583.2 127.0 %collective-permute-start.3 = (bf16[512,384]{1,0:T(8,128)(2,1)}, bf16[512,384]{1,0:T(8,128)(2,1)S(1)}, u32[]{:S(2)}, u32[]{:S(2)}) collective-permute-start(bf16[512,384]{1,0:T(8,128)(2,1)} %bitcast.258), channel_id=1, source_target_pairs={{0,0},{4,1},{8,2},{12,3},{16,4},{20,5},{24,6},{28,7},{1,8},{5,9},{... | collective-permute-start | bytes 1179656 | tf_op jit(solution)/shard_map/ppermute | solution.py:117
  707.4 3.8 collective-permute-start.2
  (51 other events, 1932.4 us)
Sparse Core Ops, SparseCore 0:
  10.2 33.3 all-gather.26
  45.4 43.8 all-gather.12
  91.0 31.6 all-gather.14
  148.6 49.9 reduce-scatter.12
  200.6 38.2 all-gather.28
  240.4 37.1 all-gather.20
  280.0 42.8 all-gather.16
  324.5 38.2 all-gather.18
  364.7 42.8 all-gather.22
  428.3 43.9 reduce-scatter.16
  477.6 43.9 all-gather.24
  523.7 40.3 reduce-scatter.28
  566.4 61.6 reduce-scatter.26
  630.3 42.4 reduce-scatter.24
  675.5 31.9 reduce-scatter.22
  709.6 34.8 reduce-scatter.20
  747.3 45.8 reduce-scatter.18
  796.0 43.9 reduce-scatter.14
  845.1 95.4 reduce-scatter.30

commit v2 on v1

v2 whole, which is shorter than its diff:
```python
import functools
import math

import jax
import jax.numpy as jnp
from jax import lax
from jax.experimental import pallas as pl
from jax.experimental.pallas import tpu as pltpu
from jax.sharding import PartitionSpec as P

HEAD_DIM = 96
EPSILON = 1e-05
ROPE_BASE = 100000.0
NEGATIVE = -1e30
SCALE = 1.0 / math.sqrt(HEAD_DIM)
MESH = pl.DeviceIdType.MESH
BLOCK = 256
F32 = jnp.float32
BF16 = jnp.bfloat16
ANY = pl.BlockSpec(memory_space=pl.ANY)
VMEM = pl.BlockSpec(memory_space=pltpu.VMEM)


def dot(left, right):
    return jnp.dot(left, right, preferred_element_type=F32)


def dot_nt(left, right):
    return lax.dot_general(left, right, (((1,), (1,)), ((), ())), preferred_element_type=F32)


def dot_tn(left, right):
    return lax.dot_general(left, right, (((0,), (0,)), ((), ())), preferred_element_type=F32)


def shape(dims, kind):
    return jax.ShapeDtypeStruct(dims, kind)


def params(collective=None):
    return pltpu.CompilerParams(
        collective_id=collective,
        has_side_effects=collective is not None,
        vmem_limit_bytes=60 << 20,
    )


def cost(flops, moved):
    return pl.CostEstimate(flops=flops, bytes_accessed=moved, transcendentals=0)


def others(size):
    me = lax.axis_index("seq")
    if size == 4:
        low, high = lax.rem(me, 2), me // 2
        return [high * 2 + 1 - low, (1 - high) * 2 + low, (1 - high) * 2 + 1 - low]
    return [lax.rem(me + step, size) for step in range(1, size)]


def meet(size, axis="seq", ends=True):
    barrier = pltpu.get_barrier_semaphore()
    for peer in others(size):
        pl.semaphore_signal(barrier, inc=1, device_id={"seq": peer}, device_id_type=MESH)
    if ends:
        pl.semaphore_wait(barrier, size - 1)


def push(src, dst, sems, index, peer, axis="seq"):
    return pltpu.make_async_remote_copy(
        src_ref=src,
        dst_ref=dst,
        send_sem=sems[0].at[index],
        recv_sem=sems[1].at[index],
        device_id={axis: peer},
        device_id_type=MESH,
    )


def n_copies(size):
    return 6 if size == 4 else size - 1


class Gather:
    def __init__(self, size, own, whole, sems):
        self.size, self.own, self.whole, self.sems = size, own, whole, sems
        self.me = lax.axis_index("seq")
        self.peers = others(size)
        half = own.shape[0] // 2
        self.parts = [pl.ds(0, half), pl.ds(half, half)]

    def copy(self, index):
        me, own, whole, sems = self.me, self.own, self.whole, self.sems
        if self.size != 4:
            return push(own, whole.at[me], sems, index, self.peers[index])
        side, over, _ = self.peers
        one, two = self.parts
        src, dst, peer = [
            (own.at[one], whole.at[me, one], side),
            (own.at[two], whole.at[me, two], side),
            (own.at[two], whole.at[me, two], over),
            (own.at[one], whole.at[me, one], over),
            (whole.at[side, one], whole.at[side, one], over),
            (whole.at[over, two], whole.at[over, two], side),
        ][index]
        return push(src, dst, sems, index, peer)

    def start(self):
        for index in (0, 2, 1, 3) if self.size == 4 else range(self.size - 1):
            self.copy(index).start()

    def forward(self):
        if self.size == 4:
            for index in (0, 2):
                self.copy(index).wait_recv()
            self.copy(4).start()
            self.copy(5).start()

    def finish(self):
        for index in range(n_copies(self.size)):
            if self.size != 4 or index not in (0, 2):
                self.copy(index).wait_recv()
        for index in range(n_copies(self.size)):
            self.copy(index).wait_send()


def scatter_scratch(size, rows, width):
    if size == 4:
        held = [
            pltpu.VMEM((3, rows, width), BF16),
            pltpu.VMEM((2, rows // 2, width), BF16),
            pltpu.VMEM((2, rows, width), BF16),
        ]
    else:
        held = [
            pltpu.VMEM((size - 1, rows, width), BF16),
            pltpu.VMEM((1, 16, 128), BF16),
            pltpu.VMEM((size - 1, rows, width), BF16),
        ]
    return held + [pltpu.SemaphoreType.DMA((n_copies(size),))] * 2


class Scatter:
    def __init__(self, size, held, stage, got, sems):
        self.size, self.held, self.stage, self.got, self.sems = size, held, stage, got, sems
        self.peers = others(size)
        half = held.shape[1] // 2
        self.parts = [pl.ds(0, half), pl.ds(half, half)]

    def copy(self, index):
        held, stage, got, sems = self.held, self.stage, self.got, self.sems
        if self.size != 4:
            return push(held.at[index], got.at[index], sems, index, self.peers[index])
        side, over, _ = self.peers
        one, two = self.parts
        src, dst, peer = [
            (held.at[2, one], stage.at[0], side),
            (held.at[2, two], stage.at[1], over),
            (held.at[0, one], got.at[0, one], side),
            (held.at[1, two], got.at[1, two], over),
            (held.at[0, two], got.at[0, two], side),
            (held.at[1, one], got.at[1, one], over),
        ][index]
        return push(src, dst, sems, index, peer)

    def send(self, make):
        if self.size != 4:
            for k, peer in enumerate(self.peers):
                make(peer, self.held.at[k])
                self.copy(k).start()
            return
        make(self.peers[2], self.held.at[2])
        self.copy(0).start()
        self.copy(1).start()
        make(self.peers[0], self.held.at[0])
        self.copy(2).start()
        make(self.peers[1], self.held.at[1])
        self.copy(3).start()

    def forward(self):
        if self.size == 4:
            one, two = self.parts
            held, stage = self.held, self.stage
            self.copy(1).wait_recv()
            held[0, two] = (held[0, two].astype(F32) + stage[1].astype(F32)).astype(BF16)
            self.copy(4).start()
            self.copy(0).wait_recv()
            held[1, one] = (held[1, one].astype(F32) + stage[0].astype(F32)).astype(BF16)
            self.copy(5).start()

    def finish(self):
        for index in range(n_copies(self.size)):
            if self.size != 4 or index > 1:
                self.copy(index).wait_recv()
        for index in range(n_copies(self.size)):
            self.copy(index).wait_send()

    def terms(self, rows):
        total = self.got[0, rows].astype(F32)
        for k in range(1, self.got.shape[0]):
            total = total + self.got[k, rows].astype(F32)
        return total


def each(count, step, task):
    def run(index, carry):
        task(pl.multiple_of(index * step, step))
        return carry

    lax.fori_loop(0, count // step, run, 0)


def tile_of(width, most):
    tile = most
    while width % tile:
        tile //= 2
    return tile


def enter_kernel(seq, fsdp, hidden, ids, gains, hidden_all, ids_all, gains_all, *sems):
    block_sems, id_sems, gain_sems, wide_sems, local = (
        sems[0:2],
        sems[2:4],
        sems[4:6],
        sems[6:8],
        sems[8],
    )
    me, row = lax.axis_index("seq"), lax.axis_index("fsdp")
    barrier = pltpu.get_barrier_semaphore()
    for peer in others(seq):
        pl.semaphore_signal(barrier, inc=1, device_id={"seq": peer}, device_id_type=MESH)
    for step in range(1, fsdp):
        pl.semaphore_signal(
            barrier,
            inc=1,
            device_id={"fsdp": lax.rem(row + step, fsdp)},
            device_id_type=MESH,
        )
    pl.semaphore_wait(barrier, seq - 1 + fsdp - 1)
    whole = Gather(seq, hidden, hidden_all, block_sems)
    small = [push(ids, ids_all.at[me], id_sems, k, peer) for k, peer in enumerate(others(seq))]
    small += [
        push(gains, gains_all.at[row, me], gain_sems, k, peer)
        for k, peer in enumerate(others(seq))
    ]
    for copy in small:
        copy.start()
    whole.start()
    kept = [
        pltpu.make_async_copy(hidden, hidden_all.at[me], local.at[0]),
        pltpu.make_async_copy(ids, ids_all.at[me], local.at[1]),
        pltpu.make_async_copy(gains, gains_all.at[row, me], local.at[2]),
    ]
    for copy in kept:
        copy.start()
    for copy in small:
        copy.wait()
    for copy in kept:
        copy.wait()
    wide = [
        push(
            gains_all.at[row],
            gains_all.at[row],
            wide_sems,
            step - 1,
            lax.rem(row + step, fsdp),
            axis="fsdp",
        )
        for step in range(1, fsdp)
    ]
    for copy in wide:
        copy.start()
    whole.forward()
    for copy in wide:
        copy.wait()
    whole.finish()


def enter(seq, fsdp, hidden, ids, gains):
    rows, width = hidden.shape
    dma = pltpu.SemaphoreType.DMA
    return pl.pallas_call(
        functools.partial(enter_kernel, seq, fsdp),
        out_shape=(
            shape((seq, rows, width), BF16),
            shape((seq, 1, rows), jnp.int32),
            shape((fsdp, seq) + gains.shape, BF16),
        ),
        in_specs=[ANY] * 3,
        out_specs=(ANY,) * 3,
        scratch_shapes=[dma((n_copies(seq),))] * 2
        + [dma((seq - 1,))] * 4
        + [dma((fsdp - 1,))] * 2
        + [dma((3,))],
        compiler_params=params(0),
        name="enter",
    )(hidden, ids, gains)


def swap_halves(block):
    half = HEAD_DIM // 2
    return jnp.concatenate([block[:, half:], block[:, :half]], axis=1)


def mask_bias(ids_col, ids_row, start, low, high):
    span = high - low
    query = start + lax.broadcasted_iota(jnp.int32, (BLOCK, span), 0)
    key = low + lax.broadcasted_iota(jnp.int32, (BLOCK, span), 1)
    same = ids_col[pl.ds(start, BLOCK), :] == ids_row[:, low:high]
    bias = jnp.where(jnp.logical_and(same, key <= query), 0.0, NEGATIVE)
    return jnp.concatenate([bias, bias], axis=0)


def key_range(start, length):
    return max(0, start - length // 2), start + BLOCK


def attend_kernel(
    seq, hidden, gain, ids_col, ids_row, cosine, sine, w_qkv, cot, normed, packed, attn, lse,
    cot_all, *sems
):
    length = hidden.shape[0]
    groups = w_qkv.shape[1] // (4 * HEAD_DIM)
    meet(seq)
    whole = Gather(seq, cot, cot_all, sems[:2])
    whole.start()
    own = pltpu.make_async_copy(cot, cot_all.at[lax.axis_index("seq")], sems[2].at[0])
    own.start()

    def norm(at):
        rows = pl.ds(at, BLOCK)
        values = hidden[rows, :].astype(F32)
        scale = lax.rsqrt(jnp.mean(values * values, axis=-1, keepdims=True) + EPSILON)
        normed[rows, :] = (values * scale * gain[...]).astype(BF16)

    each(length, BLOCK, norm)
    for group in range(groups):

        def project(at, group=group):
            rows = pl.ds(at, 512)
            low = group * 4 * HEAD_DIM
            proj = dot(normed[rows, :], w_qkv[:, low : low + 4 * HEAD_DIM])
            for slot in range(4):
                part = proj[:, slot * HEAD_DIM : (slot + 1) * HEAD_DIM]
                if slot < 3:
                    part = part * cosine[rows, :] + swap_halves(part) * sine[rows, :]
                packed[group * 4 + slot, rows, :] = part.astype(BF16)

        each(length, 512, project)
    whole.forward()
    for start in range(0, length, BLOCK):
        low, high = key_range(start, length)
        rows = pl.ds(start, BLOCK)
        keys = pl.ds(low, high - low)
        bias = mask_bias(ids_col, ids_row, start, low, high)
        mixed, logs = [], []
        for group in range(groups):
            queries = jnp.concatenate(
                [packed[group * 4, rows, :], packed[group * 4 + 1, rows, :]], axis=0
            )
            scores = dot_nt(queries, packed[group * 4 + 2, keys, :]) * SCALE + bias
            most = jnp.max(scores, axis=-1, keepdims=True)
            grown = jnp.exp(scores - most)
            total = jnp.sum(grown, axis=-1, keepdims=True)
            weights = (grown * (1.0 / total)).astype(BF16)
            out = dot(weights, packed[group * 4 + 3, keys, :])
            log_total = most + jnp.log(total)
            mixed += [out[:BLOCK], out[BLOCK:]]
            logs += [log_total[:BLOCK], log_total[BLOCK:]]
        attn[rows, :] = jnp.concatenate(mixed, axis=1).astype(BF16)
        lane = lax.broadcasted_iota(jnp.int32, (BLOCK, 128), 1)
        stats = jnp.zeros((BLOCK, 128), F32)
        for head, log_total in enumerate(logs):
            stats = jnp.where(lane == head, log_total, stats)
        lse[rows, :] = stats
    whole.finish()
    own.wait()


def attend(seq, hidden_all, gain, ids_col, ids_row, cosine, sine, w_qkv, cot):
    length, width = hidden_all.shape
    groups = w_qkv.shape[1] // (4 * HEAD_DIM)
    dma = pltpu.SemaphoreType.DMA
    return pl.pallas_call(
        functools.partial(attend_kernel, seq),
        out_shape=(
            shape((length, width), BF16),
            shape((groups * 4, length, HEAD_DIM), BF16),
            shape((length, groups * 2 * HEAD_DIM), BF16),
            shape((length, 128), F32),
            shape((seq,) + cot.shape, BF16),
        ),
        in_specs=[VMEM] * 7 + [ANY],
        out_specs=(VMEM,) * 4 + (ANY,),
        scratch_shapes=[dma((n_copies(seq),))] * 2 + [dma((1,))],
        compiler_params=params(1),
        cost_estimate=cost(2 * length * width * w_qkv.shape[1] * 4, 20 << 20),
        name="attend",
    )(hidden_all, gain, ids_col, ids_row, cosine, sine, w_qkv, cot)


def join_blocks(blocks, seq, whole):
    ratio = blocks.shape[0] // seq
    height, width = blocks.shape[1:]
    for down in range(ratio):
        for across in range(seq):
            whole[down * height : (down + 1) * height, across * width : (across + 1) * width] = (
                blocks[down * seq + across]
            )


def middle_kernel(
    seq, attn, blocks, hidden, gain, middle, normed_all, w_out, held, stage, got, *sems
):
    rows, width = hidden.shape
    me = lax.axis_index("seq")
    tile = tile_of(width, 512)
    meet(seq, ends=False)
    join_blocks(blocks, seq, w_out)
    pl.semaphore_wait(pltpu.get_barrier_semaphore(), seq - 1)
    sums = Scatter(seq, held, stage, got, sems[:2])

    def term(device, ref):
        block = pl.ds(pl.multiple_of(device * rows, rows), rows)

        def part(at):
            ref[:, pl.ds(at, tile)] = dot(attn[block, :], w_out[:, pl.ds(at, tile)]).astype(BF16)

        each(width, tile, part)

    sums.send(term)
    block = pl.ds(pl.multiple_of(me * rows, rows), rows)

    def own(at):
        cols = pl.ds(at, tile)
        middle[:, cols] = hidden[:, cols].astype(F32) + dot(attn[block, :], w_out[:, cols])

    each(width, tile, own)
    sums.forward()
    sums.finish()

    def norm(at):
        part = pl.ds(at, 128)
        values = middle[part, :] + sums.terms(part)
        middle[part, :] = values
        scale = lax.rsqrt(jnp.mean(values * values, axis=-1, keepdims=True) + EPSILON)
        normed_all[me, part, :] = (values * scale * gain[...]).astype(BF16)

    each(rows, 128, norm)
    whole = Gather(seq, normed_all.at[me], normed_all, sems[2:4])
    whole.start()
    whole.forward()
    whole.finish()


def to_middle(seq, attn, blocks, hidden, gain):
    rows, width = hidden.shape
    dma = pltpu.SemaphoreType.DMA
    return pl.pallas_call(
        functools.partial(middle_kernel, seq),
        out_shape=(
            shape((rows, width), F32),
            shape((seq, rows, width), BF16),
            shape((attn.shape[1], width), BF16),
        ),
        in_specs=[VMEM] * 4,
        out_specs=(VMEM,) * 3,
        scratch_shapes=scatter_scratch(seq, rows, width) + [dma((n_copies(seq),))] * 2,
        compiler_params=params(2),
        cost_estimate=cost(60 << 30, 10 << 20),
        name="middle",
    )(attn, blocks, hidden, gain)


def feed_kernel(seq, normed, cot, w_gate, w_up, blocks, hid, d_gate, d_up, g_down, g_both, w_down):
    length = normed.shape[0]
    height = w_down.shape[0]
    for across in range(seq):
        width = blocks.shape[-1]
        w_down[:, across * width : (across + 1) * width] = blocks[0, across]

    def part(at):
        rows = pl.ds(at, 512)
        gate = dot(normed[rows, :], w_gate[...])
        up = dot(normed[rows, :], w_up[...])
        d_hid = dot_nt(cot[rows, :], w_down[...])
        sig = 1.0 / (1.0 + jnp.exp(-gate))
        active = gate * sig
        hid[rows, :] = (active * up).astype(BF16)
        d_gate[rows, :] = (d_hid * up * sig * (1.0 + gate * (1.0 - sig))).astype(BF16)
        d_up[rows, :] = (d_hid * active).astype(BF16)

    each(length, 512, part)
    for across in range(seq):
        width = blocks.shape[-1]
        cols = slice(across * width, (across + 1) * width)
        g_down[0, across] = dot_tn(hid[...], cot[:, cols]).astype(BF16)

    def grads(at):
        rows = pl.ds(at, 512)
        g_both[rows, :height] = dot_tn(normed[:, rows], d_gate[...]).astype(BF16)
        g_both[rows, height:] = dot_tn(normed[:, rows], d_up[...]).astype(BF16)

    each(normed.shape[1], 512, grads)


def feed(seq, normed_all, cot_all, w_gate, w_up, blocks):
    length, width = normed_all.shape
    inner = w_gate.shape[1]
    ratio = blocks.shape[0] // seq
    height, across = blocks.shape[1:]
    step = min(BLOCK, height)
    per = height // step
    blocks = blocks.reshape(ratio, seq, height, across)
    keep = pl.BlockSpec((length, width), lambda c: (0, 0), pipeline_mode=pl.Buffered(1))
    cols = pl.BlockSpec((width, step), lambda c: (0, c))
    by_col = pl.BlockSpec((length, step), lambda c: (0, c))
    by_row = pl.BlockSpec((1, seq, step, across), lambda c: (c // per, 0, c % per, 0))
    outs = pl.pallas_call(
        functools.partial(feed_kernel, seq),
        grid=(inner // step,),
        out_shape=(shape((length, inner), BF16),) * 3
        + (shape(blocks.shape, BF16), shape((width, 2 * inner), BF16)),
        in_specs=[keep, keep, cols, cols, by_row],
        out_specs=(by_col,) * 3
        + (by_row, pl.BlockSpec((width, 2 * step), lambda c: (0, c))),
        scratch_shapes=[pltpu.VMEM((step, width), BF16)],
        compiler_params=params(),
        cost_estimate=cost(12 * length * width * inner, 30 << 20),
        name="feed",
    )(normed_all, cot_all, w_gate, w_up, blocks)
    return outs, step


def back_kernel(
    seq, d_gate, d_up, w_gate, w_up, hid, blocks, middle, cot, gain, d_middle, d_low_all, d_gain,
    out_terms, held, stage, got, w_down, *sems
):
    rows, width = middle.shape
    me = lax.axis_index("seq")
    tile = tile_of(width, 512)
    meet(seq)
    sums = Scatter(seq, held, stage, got, sems[:2])

    def one(device, at):
        block = pl.ds(pl.multiple_of(device * rows, rows), rows)
        cols = pl.ds(at, tile)
        return dot_nt(d_gate[block, :], w_gate[cols, :]) + dot_nt(d_up[block, :], w_up[cols, :])

    def term(device, ref):
        def part(at):
            ref[:, pl.ds(at, tile)] = one(device, at).astype(BF16)

        each(width, tile, part)

    sums.send(term)

    def own(at):
        d_middle[:, pl.ds(at, tile)] = one(me, at)

    each(width, tile, own)
    sums.forward()
    join_blocks(blocks, seq, w_down)

    def outward(index, carry):
        block = pl.ds(pl.multiple_of(index * rows, rows), rows)
        def part(at):
            cols = pl.ds(at, tile)
            out_terms[index, :, cols] = dot(hid[block, :], w_down[:, cols]).astype(BF16)

        each(width, tile, part)
        return carry

    lax.fori_loop(0, seq, outward, 0)
    sums.finish()
    d_gain[...] = jnp.zeros_like(d_gain)

    def norm(at):
        part = pl.ds(at, 128)
        values = middle[part, :]
        grad = d_middle[part, :] + sums.terms(part)
        scale = lax.rsqrt(jnp.mean(values * values, axis=-1, keepdims=True) + EPSILON)
        weighted = grad * gain[...]
        inner = jnp.mean(weighted * values, axis=-1, keepdims=True)
        d_gain[...] += jnp.sum(grad * values * scale, axis=0, keepdims=True)
        total = cot[part, :].astype(F32) + scale * (weighted - values * (scale * scale) * inner)
        d_middle[part, :] = total
        d_low_all[me, part, :] = total.astype(BF16)

    each(rows, 128, norm)
    whole = Gather(seq, d_low_all.at[me], d_low_all, sems[2:4])
    whole.start()
    whole.forward()
    whole.finish()


def back(seq, d_gate, d_up, w_gate, w_up, hid, blocks, middle, cot, gain):
    rows, width = middle.shape
    dma = pltpu.SemaphoreType.DMA
    return pl.pallas_call(
        functools.partial(back_kernel, seq),
        out_shape=(
            shape((rows, width), F32),
            shape((seq, rows, width), BF16),
            shape((1, width), F32),
            shape((seq, rows, width), BF16),
        ),
        in_specs=[VMEM] * 9,
        out_specs=(VMEM,) * 4,
        scratch_shapes=scatter_scratch(seq, rows, width)[:3]
        + [pltpu.VMEM((hid.shape[1], width), BF16)]
        + [dma((n_copies(seq),))] * 4,
        compiler_params=params(3),
        cost_estimate=cost(60 << 30, 20 << 20),
        name="back",
    )(d_gate, d_up, w_gate, w_up, hid, blocks, middle, cot, gain)


def attend_back_kernel(
    seq, d_low, w_out, attn, packed, lse, ids_col, ids_row, cosine, sine, out_terms, middle,
    g_out, d_packed, output, held, stage, got, d_attn, d_keys, d_vals, *sems
):
    length = d_low.shape[0]
    rows_own = middle.shape[0]
    groups = packed.shape[0] // 4
    ratio = g_out.shape[0] // seq
    height, width = g_out.shape[1:]
    me = lax.axis_index("seq")
    meet(seq)
    sums = Scatter(seq, held, stage, got, sems[:2])

    def term(device, ref):
        ref[...] = out_terms[device]

    sums.send(term)

    def outer(at):
        rows = pl.ds(at, 512)
        d_attn[rows, :] = dot_nt(d_low[rows, :], w_out[...]).astype(BF16)

    each(length, 512, outer)
    for across in range(seq):
        part = dot_tn(attn[...], d_low[:, across * width : (across + 1) * width]).astype(BF16)
        for down in range(ratio):
            g_out[down * seq + across] = part[down * height : (down + 1) * height]
    sums.forward()
    d_keys[...] = jnp.zeros_like(d_keys)
    d_vals[...] = jnp.zeros_like(d_vals)
    stored = [[] for _ in range(groups)]
    for start in range(0, length, BLOCK):
        low, high = key_range(start, length)
        rows = pl.ds(start, BLOCK)
        keys = pl.ds(low, high - low)
        bias = mask_bias(ids_col, ids_row, start, low, high)
        for group in range(groups):
            base = group * 2 * HEAD_DIM
            queries = jnp.concatenate(
                [packed[group * 4, rows, :], packed[group * 4 + 1, rows, :]], axis=0
            )
            mixed = attn[rows, base : base + 2 * HEAD_DIM].astype(F32)
            d_wide = d_attn[rows, base : base + 2 * HEAD_DIM]
            product = mixed * d_wide.astype(F32)
            delta = jnp.concatenate(
                [
                    jnp.sum(product[:, :HEAD_DIM], axis=-1, keepdims=True),
                    jnp.sum(product[:, HEAD_DIM:], axis=-1, keepdims=True),
                ],
                axis=0,
            )
            d_out = jnp.concatenate([d_wide[:, :HEAD_DIM], d_wide[:, HEAD_DIM:]], axis=0)
            logs = jnp.concatenate(
                [
                    lse[rows, group * 2 : group * 2 + 1],
                    lse[rows, group * 2 + 1 : group * 2 + 2],
                ],
                axis=0,
            )
            key_rows = packed[group * 4 + 2, keys, :]
            scores = dot_nt(queries, key_rows) * SCALE + bias
            probs = jnp.exp(scores - logs)
            d_probs = dot_nt(d_out, packed[group * 4 + 3, keys, :])
            d_scores = (probs * (d_probs - delta)).astype(BF16)
            d_vals[group, keys, :] += dot_tn(probs.astype(BF16), d_out)
            d_keys[group, keys, :] += dot_tn(d_scores, queries) * SCALE
            d_query = dot(d_scores, key_rows) * SCALE
            turned = [
                part * cosine[rows, :] - swap_halves(part) * sine[rows, :]
                for part in (d_query[:BLOCK], d_query[BLOCK:])
            ]
            d_packed[rows, group * 4 * HEAD_DIM : group * 4 * HEAD_DIM + 2 * HEAD_DIM] = (
                jnp.concatenate(turned, axis=1).astype(BF16)
            )

    def last(at):
        rows = pl.ds(at, BLOCK)
        for group in range(groups):
            d_key = d_keys[group, rows, :]
            turned = d_key * cosine[rows, :] - swap_halves(d_key) * sine[rows, :]
            base = group * 4 * HEAD_DIM + 2 * HEAD_DIM
            d_packed[rows, base : base + 2 * HEAD_DIM] = jnp.concatenate(
                [turned, d_vals[group, rows, :]], axis=1
            ).astype(BF16)

    each(length, BLOCK, last)
    sums.finish()

    def total(at):
        part = pl.ds(at, 128)
        output[part, :] = middle[part, :] + out_terms[me, part, :].astype(F32) + sums.terms(part)

    each(rows_own, 128, total)


def attend_back(
    seq, fsdp, d_low_all, w_out, attn, packed, lse, ids_col, ids_row, cosine, sine, out_terms, middle
):
    rows, width = middle.shape
    length = d_low_all.shape[0]
    inner = attn.shape[1]
    groups = packed.shape[0] // 4
    height = inner // (fsdp // seq)
    return pl.pallas_call(
        functools.partial(attend_back_kernel, seq),
        out_shape=(
            shape((fsdp, height, width // seq), BF16),
            shape((length, groups * 4 * HEAD_DIM), BF16),
            shape((rows, width), F32),
        ),
        in_specs=[VMEM] * 11,
        out_specs=(VMEM,) * 3,
        scratch_shapes=scatter_scratch(seq, rows, width)[:3]
        + [pltpu.VMEM((length, inner), BF16)]
        + [pltpu.VMEM((groups, length, HEAD_DIM), F32)] * 2
        + [pltpu.SemaphoreType.DMA((n_copies(seq),))] * 2,
        compiler_params=params(4),
        cost_estimate=cost(30 << 30, 20 << 20),
        name="attend_back",
    )(d_low_all, w_out, attn, packed, lse, ids_col, ids_row, cosine, sine, out_terms, middle)


def leave_kernel(
    seq, d_packed, w_qkv, hidden, d_middle, gain, d_input, d_gain, held, stage, got, *sems
):
    rows, width = hidden.shape
    me = lax.axis_index("seq")
    tile = tile_of(width, 512)
    meet(seq)
    sums = Scatter(seq, held, stage, got, sems[:2])

    def one(device, at):
        block = pl.ds(pl.multiple_of(device * rows, rows), rows)
        return dot_nt(d_packed[block, :], w_qkv[pl.ds(at, tile), :])

    def term(device, ref):
        def part(at):
            ref[:, pl.ds(at, tile)] = one(device, at).astype(BF16)

        each(width, tile, part)

    sums.send(term)

    def own(at):
        d_input[:, pl.ds(at, tile)] = one(me, at)

    each(width, tile, own)
    sums.forward()
    sums.finish()
    d_gain[...] = jnp.zeros_like(d_gain)

    def norm(at):
        part = pl.ds(at, 128)
        values = hidden[part, :].astype(F32)
        grad = d_input[part, :] + sums.terms(part)
        scale = lax.rsqrt(jnp.mean(values * values, axis=-1, keepdims=True) + EPSILON)
        weighted = grad * gain[...]
        inner = jnp.mean(weighted * values, axis=-1, keepdims=True)
        d_gain[...] += jnp.sum(grad * values * scale, axis=0, keepdims=True)
        d_input[part, :] = d_middle[part, :] + scale * (
            weighted - values * (scale * scale) * inner
        )

    each(rows, 128, norm)


def leave(seq, d_packed, w_qkv, hidden, d_middle, gain):
    rows, width = hidden.shape
    return pl.pallas_call(
        functools.partial(leave_kernel, seq),
        out_shape=(shape((rows, width), F32), shape((1, width), F32)),
        in_specs=[VMEM] * 5,
        out_specs=(VMEM,) * 2,
        scratch_shapes=scatter_scratch(seq, rows, width),
        compiler_params=params(5),
        cost_estimate=cost(30 << 30, 10 << 20),
        name="leave",
    )(d_packed, w_qkv, hidden, d_middle, gain)


def rope_tables(ids):
    length = ids.shape[0]
    first = jnp.sum((ids[None, :] < ids[:, None]).astype(jnp.int32), axis=1)
    positions = jnp.arange(length, dtype=jnp.int32) - first
    half_dim = HEAD_DIM // 2
    freq_steps = jnp.arange(half_dim, dtype=F32)
    inverse = jnp.exp(freq_steps * (-2.0 * math.log(ROPE_BASE) / HEAD_DIM))
    angles = positions.astype(F32)[:, None] * inverse[None, :]
    cosine, sine = jnp.cos(angles), jnp.sin(angles)
    return (
        jnp.concatenate([cosine, cosine], axis=1),
        jnp.concatenate([-sine, sine], axis=1),
    )


def body(
    hidden_in, cotangent, segment_ids, w_qkv, w_out, w_gate, w_up, w_down, gain_attn, gain_mlp
):
    rows, width = hidden_in.shape
    fsdp = lax.axis_size("fsdp")
    seq = lax.axis_size("seq")
    ratio = fsdp // seq
    length = rows * seq
    moves = [
        (f * seq + s, ((f % ratio) * seq + s) * seq + f // ratio)
        for f in range(fsdp)
        for s in range(seq)
    ]
    home = [(there, here) for here, there in moves]

    def gather_cols(shard):
        return lax.all_gather(shard, "fsdp", axis=0, tiled=True)

    def gather_rows(shard):
        moved = lax.ppermute(shard, ("fsdp", "seq"), moves)
        return lax.all_gather(moved, "fsdp", axis=0, tiled=False)

    def scatter_cols(grad):
        return lax.psum_scatter(grad, "fsdp", scatter_dimension=0, tiled=True)

    def scatter_rows(blocks):
        own = lax.psum_scatter(blocks, "fsdp", scatter_dimension=0, tiled=False)
        return lax.ppermute(own, ("fsdp", "seq"), home).astype(F32)

    cols_qkv = gather_cols(w_qkv)
    blocks_out = gather_rows(w_out)
    cols_gate = gather_cols(w_gate)
    cols_up = gather_cols(w_up)
    blocks_down = gather_rows(w_down)

    hidden_all, ids_all, gains = enter(
        seq, fsdp, hidden_in, segment_ids, jnp.stack([gain_attn, gain_mlp])
    )
    gains = jnp.transpose(gains, (2, 0, 1, 3)).reshape(2, width).astype(F32)
    gain_one, gain_two = gains[:1], gains[1:]
    ids_row = ids_all.reshape(1, length)
    ids_col = ids_all.reshape(length, 1)
    cosine, sine = rope_tables(ids_all.reshape(length))

    normed_one, packed, attn, lse, cot_all = attend(
        seq, hidden_all.reshape(length, width), gain_one, ids_col, ids_row, cosine, sine,
        cols_qkv, cotangent,
    )
    cot_all = cot_all.reshape(length, width)
    middle, normed_two, rows_out = to_middle(seq, attn, blocks_out, hidden_in, gain_two)
    normed_two = normed_two.reshape(length, width)
    (hid, d_gate, d_up, g_down, g_both), step = feed(
        seq, normed_two, cot_all, cols_gate, cols_up, blocks_down
    )
    g_both = scatter_cols(g_both)
    g_down = scatter_rows(g_down.reshape(blocks_down.shape))
    d_middle, d_low_all, part_two, out_terms = back(
        seq, d_gate, d_up, cols_gate, cols_up, hid, blocks_down, middle, cotangent, gain_two
    )
    g_out, d_packed, output = attend_back(
        seq, fsdp, d_low_all.reshape(length, width), rows_out, attn, packed, lse, ids_col, ids_row,
        cosine, sine, out_terms, middle,
    )
    g_qkv = dot_tn(normed_one, d_packed).astype(BF16)
    g_out = scatter_rows(g_out)
    g_qkv = scatter_cols(g_qkv).astype(F32)
    d_tokens, part_one = leave(seq, d_packed, cols_qkv, hidden_in, d_middle, gain_one)
    totals = lax.psum(jnp.concatenate([part_one, part_two], axis=0), ("fsdp", "seq"))
    share = width // (fsdp * seq)
    at = (lax.axis_index("fsdp") * seq + lax.axis_index("seq")) * share
    g_gains = lax.dynamic_slice_in_dim(totals, at, share, 1)
    g_both = g_both.reshape(g_both.shape[0], -1, 2, step).astype(F32)
    g_gate = g_both[:, :, 0].reshape(g_both.shape[0], -1)
    g_up = g_both[:, :, 1].reshape(g_both.shape[0], -1)
    return (output, d_tokens, g_qkv, g_out, g_gate, g_up, g_down, g_gains[0], g_gains[1])


def solution(mesh):
    both = P(("fsdp", "seq"), None)
    split = P("fsdp", "seq")
    gain = P(("fsdp", "seq"))
    in_specs = (both, both, split, split, split, split, split, split, gain, gain)
    out_specs = (both, both, split, split, split, split, split, gain, gain)
    return jax.shard_map(body, mesh=mesh, in_specs=in_specs, out_specs=out_specs, check_vma=False)
```

time: 960 us -> 527 us (0.55)
  waiting for transfers between devices: 643 us -> 91.3 us
  Pallas kernels: 0 us -> 316 us
  matrix products: 134 us -> 5.45 us
  other arithmetic: 34.8 us -> 10.6 us
  blocking collectives: 81.8 us -> 58.1 us
  local copies, waits for them, and re-layouts: 34.7 us -> 16.7 us
    pallas_call x0 -> x7, Pallas kernels: none -> 316 us  [the longest x1 69.8 us: back(): pl.pallas_call(functools.partial(back_kernel, seq), out_shape=(shape((row...]
    reduce_scatter x7 -> x2, waiting for transfers between devices: 299 us -> 61.3 us  [scatter_cols(): return lax.psum_scatter(grad, 'fsdp', scatter_dimension=0, tiled=True)]
    dot_general x27 -> x1, matrix products: 134 us -> 5.45 us  [dot_tn(): lax.dot_general(left, right, (((0,), (0,)), ((), ())), preferred_element_...]
    all_gather x6 -> x2, waiting for transfers between devices: 127 us -> 27.3 us  [gather_rows(): return lax.all_gather(moved, 'fsdp', axis=0, tiled=False)]
    unnamed x20 -> x9, waiting for transfers between devices: 100 us -> 2.65 us
    all_gather x3, waiting for transfers between devices: 83.8 us -> 0.06 us  [gather_cols(): return lax.all_gather(shard, 'fsdp', axis=0, tiled=True)]
    all_gather x2 -> x0, blocking collectives: 81.8 us -> none  [the longest x1 74.6 us: body(): lax.all_gather(jnp.stack([gain_attn, gain_mlp]), ('fsdp', 'seq'), axis=1,...]
    psum x0 -> x1, blocking collectives: none -> 58.1 us  [body(): lax.psum(jnp.concatenate([part_one, part_two], axis=0), ('fsdp', 'seq'))]
  transfers between devices with their start and end apart: 23 -> 13, of which waited for: 16 -> 2; matrix products, arithmetic and copies ran while one was open for 15% -> 4% of each run, Pallas kernels for 0% -> 55%
where the time goes in v2:
time: 527 us; the launch traced here: 520 us
  Pallas kernels  316 us (60%)
  waiting for transfers between devices  91.3 us (17%)
  blocking collectives  58.1 us (11%)
  local copies, waits for them, and re-layouts  16.7 us (3%)
  between operations  14.2 us (3%)
  other arithmetic  10.6 us (2%)
  starting transfers between devices  6.96 us (1%)
  matrix products  5.45 us (1%)
    pallas_call x1, Pallas kernels, back(): pl.pallas_call(functools.partial(back_kernel, seq), out_shape=(shape((row...  69.8 us
    reduce_scatter x2, waiting for transfers between devices, scatter_cols(): return lax.psum_scatter(grad, 'fsdp', scatter_dimension=0, tiled=True)  61.3 us
    pallas_call x1, Pallas kernels, to_middle(): pl.pallas_call(functools.partial(middle_kernel, seq), out_shape=(shape((r...  58.1 us
    psum x1, blocking collectives, body(): lax.psum(jnp.concatenate([part_one, part_two], axis=0), ('fsdp', 'seq'))  58.1 us
    pallas_call x1, Pallas kernels, enter(): pl.pallas_call(functools.partial(enter_kernel, seq, fsdp), out_shape=(sha...  52.6 us
    pallas_call x1, Pallas kernels, attend(): pl.pallas_call(functools.partial(attend_kernel, seq), out_shape=(shape((l...  35.7 us
    pallas_call x1, Pallas kernels, attend_back(): pl.pallas_call(functools.partial(attend_back_kernel, seq), out_shape=(sha...  34.9 us
    pallas_call x1, Pallas kernels, leave(): pl.pallas_call(functools.partial(leave_kernel, seq), out_shape=(shape((ro...  33.2 us
  transfers between devices with their start and end apart: 13, of which 2 were waited for; matrix products, arithmetic and copies ran while one was open for 4% of the time, Pallas kernels for 55%

profile of v2, /device:TPU:0, one launch (start us, length us, event | category | flops | bytes accessed | tf_op | source)
XLA Modules:
  0.0 519.7 jit_solution(12542367852522494872)
XLA Ops:
  8.0 1.6 collective-permute-start
  11.6 1.7 collective-permute-start.1
  13.2 1.2 pad_maximum_fusion.3.gains
  14.4 52.6 %enter.1 = (bf16[4,256,1536]{2,1,0:T(8,128)(2,1)}, s32[4,1,256]{2,1,0:T(1,128)}, bf16[8,4,2,48]{3,2,1,0:T(2,128)(2,1)}) custom-call(bf16[256,1536]{1,0:T(8,128)(2,1)} %hidden.5, s32[1,256]{1,0:T(1,128)} %ids.1, bf16[2,48]{1,0:T(2,128)(2,1)} %pad_maximum_fusion.3.gains), custom_call_target="tpu_custom_call" | custom-call | tf_op jit(solution)/shard_map/enter/pallas_call | solution.py:281
  67.1 1.7 copy.21.ids_col
  71.0 1.3 convert_reduce_fusion
  72.3 1.9 fusion
  74.2 1.3 pad_maximum_fusion
  76.6 35.7 %attend.1 = (bf16[1024,1536]{1,0:T(8,128)(2,1)}, bf16[8,1024,96]{2,1,0:T(8,128)(2,1)}, bf16[1024,384]{1,0:T(8,128)(2,1)}, f32[1024,128]{1,0:T(8,128)}, bf16[4,256,1536]{2,1,0:T(8,128)(2,1)}) custom-call(bf16[1024,1536]{1,0:T(8,128)(2,1)} %bitcast.38, f32[1,1536]{1,0:T(1,128)} %slice.25.gain, s32[1024,1]{1,0:T(8,128)} %copy.21.ids_col, s32[1,1024]{1,0:T(1,128)} %bitcast.34, ...), custom_call_target="tpu_custom_call" | custom-call | flops 9663676416 | bytes 20971520 | tf_op jit(solution)/shard_map/attend/pallas_call | solution.py:383
  112.3 58.1 %middle.1 = (f32[256,1536]{1,0:T(8,128)}, bf16[4,256,1536]{2,1,0:T(8,128)(2,1)}, bf16[384,1536]{1,0:T(8,128)(2,1)}) custom-call(bf16[1024,384]{1,0:T(8,128)(2,1)} %get-tuple-element.37.attn, bf16[8,192,384]{2,1,0:T(8,128)(2,1)} %bitcast.39, bf16[256,1536]{1,0:T(8,128)(2,1)} %hidden.5, f32[1,1536]{1,0:T(1,128)} %slice.27.gain), custom_call_target="tpu_custom_call" | custom-call | flops 64424509440 | bytes 10485760 | tf_op jit(solution)/shard_map/middle/pallas_call | solution.py:458
  170.5 27.3 %all-gather.16.cloned.1.call-done = bf16[4096,384]{1,0:T(8,128)(2,1)} async-done(((bf16[512,384]{1,0:T(8,128)(2,1)}), bf16[4096,384]{1,0:T(8,128)(2,1)}) %all-gather.16.cloned.1.call-update) | async-done | bytes 3145744 | tf_op jit(solution)/shard_map/all_gather | solution.py:833
  197.7 32.0 %feed.1 = (bf16[1024,1024]{1,0:T(8,128)(2,1)}, bf16[1024,1024]{1,0:T(8,128)(2,1)}, bf16[1024,1024]{1,0:T(8,128)(2,1)}, bf16[2,4,512,384]{3,2,1,0:T(8,128)(2,1)}, bf16[1536,2048]{1,0:T(8,128)(2,1)}) custom-call(bf16[1024,1536]{1,0:T(8,128)(2,1)} %bitcast.46, bf16[1024,1536]{1,0:T(8,128)(2,1)} %bitcast.44, ...), custom_call_target="tpu_custom_call" | custom-call | flops 19327352832 | bytes 31457280 | tf_op jit(solution)/shard_map/feed/pallas_call | solution.py:518
  229.7 69.8 %back.1 = (f32[256,1536]{1,0:T(8,128)}, bf16[4,256,1536]{2,1,0:T(8,128)(2,1)}, f32[1,1536]{1,0:T(1,128)}, bf16[4,256,1536]{2,1,0:T(8,128)(2,1)}) custom-call(bf16[1024,1024]{1,0:T(8,128)(2,1)} %get-tuple-element.40.d_gate, bf16[1024,1024]{1,0:T(8,128)(2,1)} %get-tuple-element.41.d_up, bf16[1536,1024]{1,0:T(8,128)(2,1)} %all-gather.10.cloned.1.call-done.w_gate, ...), custom_call_target="tpu_custom_call" | custom-call | flops 64424509440 | bytes 20971520 | tf_op jit(solution)/shard_map/back/pallas_call | solution.py:599
  299.5 34.9 %attend_back.1 = (bf16[8,192,384]{2,1,0:T(8,128)(2,1)}, bf16[1024,768]{1,0:T(8,128)(2,1)}, f32[256,1536]{1,0:T(8,128)}) custom-call(bf16[1024,1536]{1,0:T(8,128)(2,1)} %bitcast.45, bf16[384,1536]{1,0:T(8,128)(2,1)} %get-tuple-element.45.w_out, bf16[1024,384]{1,0:T(8,128)(2,1)} %get-tuple-element.37.attn, bf16[8,1024,96]{2,1,0:T(8,128)(2,1)} %get-tuple-element.46.packed, ...), custom_call_target="tpu_custom_call" | custom-call | flops 32212254720 | bytes 20971520 | tf_op jit(solution)/shard_map/attend_back/pallas_call | solution.py:721
  334.5 5.5 %convolution_convert_fusion = bf16[1536,768]{1,0:T(8,128)(2,1)} fusion(bf16[1024,1536]{1,0:T(8,128)(2,1)S(1)} %copy-done.5, bf16[1024,768]{1,0:T(8,128)(2,1)} %get-tuple-element.50.d_packed), kind=kOutput, calls=%fused_computation.1 | convolution fusion | flops 2417098752 | bytes 7077888 | tf_op jit(solution)/shard_map/dot_general | solution.py:33
  340.8 33.2 %leave.1 = (f32[256,1536]{1,0:T(8,128)}, f32[1,1536]{1,0:T(1,128)}) custom-call(bf16[1024,768]{1,0:T(8,128)(2,1)} %get-tuple-element.50.d_packed, bf16[1536,768]{1,0:T(8,128)(2,1)} %all-gather.8.cloned.1.call-done.w_qkv, bf16[256,1536]{1,0:T(8,128)(2,1)} %hidden.5, f32[256,1536]{1,0:T(8,128)} %get-tuple-element.51.d_middle, f32[1,1536]{1,0:T(1,128)} %slice.25.gain), custom_call_target="tpu_custom_call" | custom-call | flops 32212254720 | bytes 10485760 | tf_op jit(solution)/shard_map/leave/pallas_call | solution.py:786
  374.1 1.7 collective-permute-start.3
  376.4 58.1 %psum.7 = f32[2,1536]{1,0:T(2,128)S(1)} all-reduce(f32[2,1536]{1,0:T(2,128)S(1)} %pad_maximum_fusion.2), channel_id=1, replica_groups=mesh['fsdp'=8,'seq'=4] {'fsdp','seq'}, use_global_device_ids=true, to_apply=%region_5.0 | all-reduce | flops 3072 | bytes 24576 | tf_op jit(solution)/shard_map/psum | solution.py:880
  434.6 1.6 collective-permute-start.2
  437.4 1.8 convert_element_type.40
  440.1 61.3 %reduce-scatter.9.cloned.1.call-done = bf16[192,2048]{1,0:T(8,128)(2,1)} async-done(((bf16[1536,2048]{1,0:T(8,128)(2,1)}), bf16[192,2048]{1,0:T(8,128)(2,1)}) %reduce-scatter.9.cloned.1.call-update) | async-done | bytes 786448 | tf_op jit(solution)/shard_map/reduce_scatter | solution.py:836
  501.4 2.7 reshape.71
  504.2 4.5 slice_reduce_fusion
  510.7 1.1 copy.27
  (55 shorter events, 13.1 us)
Async XLA Ops:
  7.2 69.4 %all-gather.8.cloned.1.call-start = ((), (), s32[]{:S(2)}) async-start(), calls=%async_computation.4 | async-start | bytes 2654208 | tf_op jit(solution)/shard_map/all_gather | solution.py:829
  7.9 104.4 %all-gather.14.cloned.1.call-start = ((), (), s32[]{:S(2)}) async-start(), calls=%async_computation.11 | async-start | bytes 1327104 | tf_op jit(solution)/shard_map/all_gather | solution.py:833
  8.0 1.6 collective-permute-start
  9.5 0.7 copy-start.3
  10.2 160.2 %all-gather.10.cloned.1.call-start = ((), (), s32[]{:S(2)}) async-start(), calls=%async_computation.5 | async-start | bytes 3538944 | tf_op jit(solution)/shard_map/all_gather | solution.py:829
  11.0 159.5 %all-gather.12.cloned.1.call-start = ((), (), s32[]{:S(2)}) async-start(), calls=%async_computation.6 | async-start | bytes 3538944 | tf_op jit(solution)/shard_map/all_gather | solution.py:829
  11.5 186.2 %all-gather.16.cloned.1.call-start = ((), (), s32[]{:S(2)}) async-start(), calls=%async_computation.12 | async-start | bytes 3538944 | tf_op jit(solution)/shard_map/all_gather | solution.py:833
  11.6 64.0 %collective-permute-start.1 = (bf16[512,384]{1,0:T(8,128)(2,1)}, bf16[512,384]{1,0:T(8,128)(2,1)S(1)}, u32[]{:S(2)}, u32[]{:S(2)}) collective-permute-start(bf16[512,384]{1,0:T(8,128)(2,1)} %param.17), channel_id=1, source_target_pairs={{0,0},{1,4},{2,8},{3,12},{4,16},{5,20},{6,24},{7,28},{8,1},{9,5},{... | collective-permute-start | bytes 1179656 | tf_op jit(solution)/shard_map/ppermute | solution.py:832
  75.5 0.7 copy-start.2
  76.3 297.7 %reduce-scatter.11.cloned.1.call-start = ((), (), s32[]{:S(2)}) async-start(), calls=%async_computation.10 | async-start | bytes 3538944 | tf_op jit(solution)/shard_map/reduce_scatter | solution.py:839
  229.7 204.9 %reduce-scatter.7.cloned.1.call-start = ((), (), s32[]{:S(2)}) async-start(), calls=%async_computation.8 | async-start | bytes 1327104 | tf_op jit(solution)/shard_map/reduce_scatter | solution.py:839
  299.5 35.0 %copy-start.5 = (bf16[1024,1536]{1,0:T(8,128)(2,1)S(1)}, bf16[1024,1536]{1,0:T(8,128)(2,1)}, u32[]{:S(2)}) copy-start(bf16[1024,1536]{1,0:T(8,128)(2,1)} %get-tuple-element.53) | copy-start | bytes 9437188
  334.5 102.9 %reduce-scatter.5.cloned.1.call-start = ((), (), s32[]{:S(2)}) async-start(), calls=%async_computation.7 | async-start | bytes 2654208 | tf_op jit(solution)/shard_map/reduce_scatter | solution.py:836
  340.0 161.4 %reduce-scatter.9.cloned.1.call-start = ((), (), s32[]{:S(2)}) async-start(), calls=%async_computation.9 | async-start | bytes 7077888 | tf_op jit(solution)/shard_map/reduce_scatter | solution.py:836
  340.8 34.9 %copy-start.4 = (f32[1,1536]{1,0:T(1,128)S(1)}, f32[1,1536]{1,0:T(1,128)}, u32[]{:S(2)}) copy-start(f32[1,1536]{1,0:T(1,128)} %get-tuple-element.58) | copy-start | bytes 18436
  374.1 65.1 %collective-permute-start.3 = (bf16[512,384]{1,0:T(8,128)(2,1)}, bf16[512,384]{1,0:T(8,128)(2,1)S(1)}, u32[]{:S(2)}, u32[]{:S(2)}) collective-permute-start(bf16[512,384]{1,0:T(8,128)(2,1)} %bitcast.40), channel_id=1, source_target_pairs={{0,0},{4,1},{8,2},{12,3},{16,4},{20,5},{24,6},{28,7},{1,8},{5,9},{... | collective-permute-start | bytes 1179656 | tf_op jit(solution)/shard_map/ppermute | solution.py:840
  434.6 2.1 collective-permute-start.2
  508.6 2.1 copy-start
  509.7 2.2 copy-start.1
Sparse Core Ops, SparseCore 0:
  9.7 45.1 all-gather.7
  57.0 22.9 all-gather.13
  81.7 38.0 all-gather.9
  121.3 37.1 all-gather.11
  160.5 37.1 all-gather.15
  229.8 39.1 reduce-scatter.10
  334.6 30.5 reduce-scatter.6
  367.5 56.0 reduce-scatter.4
  425.9 75.5 reduce-scatter.8
